TPU v7x, 32 devices: a whole 2x2x4 slice. The times are simulated.
32 devices in a mesh: src: 16 (over z, y, x), lev: 2 (over core).
Axes of the slice: x: 2, y: 2, z: 4, core: 2. Of those that a mesh axis runs over, the one named last changes fastest.
Arguments:
- field: bfloat16 [32768, 256], P('src', 'lev'), may hold values from -6 to 6
- grad_coef: float32 [2, 4, 32768], P(None, None, 'src'), may hold values from -6 to 6
- neighbours: int32 [32768, 4], P('src'), may hold values from 0 to 2175, as said below
- level_weight: float32 [8], replicated, may hold values from 0.2 to 2
- src_index: int32 [2048, 64], P('src'), may hold values from 0 to 2047
- tgt_index: int32 [2048, 32], P('src'), may hold values from 0 to 1023
- block_dest: int32 [2048, 1], P('src'), may hold values from 0 to 15; in each aligned block of 128 rows (0 to 127, 128 to 255, ...) at most 16 rows name the same one
- weights: bfloat16 [2048, 6144], P('src'), may hold values from -0.21875 to 0.21875
Outputs:
- remapped: bfloat16 [16384, 256], P('src', 'lev')
- column_total: float32 [32, 16384], P(None, 'src')
Inputs may be any that keep to these rules, and one draw needn't show every extreme that they name: `neighbours`: position 64 + p is the device's own cell p; positions below 64 and from 2112 on are the last and first cells of the devices before and after along the closed curve; a neighbour lies at most 64 cells from the cell. `block_dest`: the 128 blocks of one index of src name one target index at most 16 times.
All inputs are finite; a program needn't handle non-finite values.
Results may differ from a plain program's by a relative error of at most 0.0049.
Values may be sent and summed in bfloat16 or wider, within the bound.
A program may use at most 128 MiB of HBM per device.

v0:
```python
import functools

import jax
import jax.numpy as jnp
from jax import lax
from jax.experimental import pallas as pl
from jax.experimental.pallas import tpu as pltpu
from jax.sharding import PartitionSpec as P

FIELDS = 32
HW = 64
SB = 64
TB = 32
T_DEV = 1024
LANES = 128
SUB = 8
TILE = 128
GROUP = LANES // TB
GROUP_BITS = GROUP.bit_length() - 1
PIECE = 32
UNROLL = 4
BATCH = 16
SPAN = SB + SUB
MESH = pl.DeviceIdType.MESH


def tag_lines(capacity):
    return -(-capacity // (GROUP * SUB)) * SUB


def contract_first(a, b):
    return lax.dot_general(a, b, (((0,), (0,)), ((), ())), preferred_element_type=jnp.float32)


def prepare_kernel(count, field_ref, coef_ref, near_ref, recon, ext, mixes, out_sem, in_sem):
    cells = field_ref.shape[0]
    window = TILE + 2 * HW
    tiles = cells // TILE
    me = lax.axis_index("src")
    lev = lax.axis_index("lev")
    right = lax.rem(me + 1, count)
    left = lax.rem(me + count - 1, count)
    barrier = pltpu.get_barrier_semaphore()
    for other in (left, right):
        pl.semaphore_signal(barrier, inc=1, device_id=(other, lev), device_id_type=MESH)
    ext[HW:HW + cells, :] = field_ref[...]

    def tile(t):
        base = pl.multiple_of(t * TILE, TILE)
        near = near_ref[:, pl.ds(base, TILE)] - base
        coef = [coef_ref[g, :, pl.ds(base, TILE)] for g in range(2)]
        totals = [-jnp.sum(coef[g], axis=0, keepdims=True) for g in range(2)]
        held = ext[pl.ds(base, window), :]
        rows = pl.multiple_of(base * SUB, TILE * SUB)
        recon[pl.ds(rows, TILE, stride=SUB), :] = field_ref[pl.ds(base, TILE), :].astype(
            jnp.float32
        )
        for w in range(0, window, PIECE):
            here = lax.broadcasted_iota(jnp.int32, (PIECE, TILE), 0) + w
            own = here == lax.broadcasted_iota(jnp.int32, (PIECE, TILE), 1) + HW
            mixed = [jnp.where(own, totals[g], 0.0) for g in range(2)]
            for k in range(near.shape[0]):
                hit = here == near[k:k + 1, :]
                for g in range(2):
                    mixed[g] = mixed[g] + jnp.where(hit, coef[g][k:k + 1, :], 0.0)
            for g in range(2):
                high = mixed[g].astype(jnp.bfloat16)
                rest = (mixed[g] - high.astype(jnp.float32)).astype(jnp.bfloat16)
                mixes[w:w + PIECE, 2 * g * TILE:(2 * g + 1) * TILE] = high
                mixes[w:w + PIECE, (2 * g + 1) * TILE:(2 * g + 2) * TILE] = rest
        for g in range(2):
            value = contract_first(mixes[:, 2 * g * TILE:(2 * g + 1) * TILE], held)
            value = value + contract_first(mixes[:, (2 * g + 1) * TILE:(2 * g + 2) * TILE], held)
            recon[pl.ds(rows + 1 + g, TILE, stride=SUB), :] = value

    @pl.loop(1, tiles // 2)
    def _(t):
        tile(t)

    pl.semaphore_wait(barrier, 2)
    low = pltpu.make_async_remote_copy(
        src_ref=field_ref.at[pl.ds(cells - HW, HW)], dst_ref=ext.at[pl.ds(0, HW)],
        send_sem=out_sem.at[0], recv_sem=in_sem.at[0],
        device_id=(right, lev), device_id_type=MESH,
    )
    high = pltpu.make_async_remote_copy(
        src_ref=field_ref.at[pl.ds(0, HW)], dst_ref=ext.at[pl.ds(HW + cells, HW)],
        send_sem=out_sem.at[1], recv_sem=in_sem.at[1],
        device_id=(left, lev), device_id_type=MESH,
    )
    low.start()
    high.start()

    @pl.loop(tiles // 2, tiles - 1)
    def _(t):
        tile(t)

    low.wait()
    high.wait()

    @pl.loop(0, 2)
    def _(e):
        tile(e * (tiles - 1))


def prepare(count, field, coef, near_t):
    cells, columns = field.shape
    vmem = pl.BlockSpec(memory_space=pltpu.VMEM)
    return pl.pallas_call(
        functools.partial(prepare_kernel, count),
        out_shape=jax.ShapeDtypeStruct((cells * SUB, columns), jnp.float32),
        in_specs=[vmem] * 3,
        out_specs=vmem,
        scratch_shapes=[
            pltpu.VMEM((cells + 2 * HW, columns), jnp.bfloat16),
            pltpu.VMEM((TILE + 2 * HW, 4 * TILE), jnp.bfloat16),
            pltpu.SemaphoreType.DMA((2,)),
            pltpu.SemaphoreType.DMA((2,)),
        ],
        compiler_params=pltpu.CompilerParams(
            vmem_limit_bytes=24 << 20, collective_id=1, has_side_effects=True
        ),
        name="prepare",
    )(field, coef, near_t)


def partial_kernel(
    capacity, src_count,
    src_ref, row_ref, tag_ref, recon, tgt_ref, weight_ref,
    send_ref,
    picked, tags,
):
    blocks = tgt_ref.shape[0]
    rows_each = capacity * TB
    lines = tags.shape[0] // src_count

    send_ref[...] = jnp.zeros_like(send_ref)
    tags[...] = jnp.zeros_like(tags)

    lane_group = lax.broadcasted_iota(jnp.int32, (1, LANES), 1) // TB

    def one(b, buffer):
        index = src_ref.at[b]
        for begin in range(0, SB, BATCH):
            found = [
                recon[pl.ds(pl.multiple_of(index[begin + j], SUB), SUB), :] for j in range(BATCH)
            ]
            for j in range(BATCH):
                to = ((begin + j) % GROUP) * (SB // GROUP) + (begin + j) // GROUP
                buffer[pl.ds(to, 3, stride=SPAN), :] = found[j][0:3, :]
        held = weight_ref[b]
        total = None
        for q in range(GROUP):
            parts = [
                buffer[pl.ds(c * SPAN + q * (SB // GROUP), SB // GROUP), :] for c in range(3)
            ]
            rows = jnp.concatenate(parts, axis=0).astype(jnp.bfloat16)
            product = contract_first(held[:, q * TB:(q + 1) * TB], rows)
            total = product if total is None else total + product
        send_ref[pl.ds(pl.multiple_of(row_ref[b], TB // 2), TB), :] = total.astype(jnp.bfloat16)
        tag = tag_ref[b]
        line = pl.ds(lax.shift_right_logical(tag, GROUP_BITS), 1)
        tags[line, :] = jnp.where(
            lane_group == jnp.bitwise_and(tag, GROUP - 1), tgt_ref[pl.ds(b, 1), :], tags[line, :]
        )

    @pl.loop(0, blocks // UNROLL)
    def _(n):
        for m in range(UNROLL):
            one(UNROLL * n + m, picked.at[m])

    @pl.loop(0, src_count)
    def _(d):
        cell = tags[pl.ds(pl.multiple_of(d * lines, SUB), lines), :]
        digits = jnp.concatenate([cell // 256, cell % 256], axis=0).astype(jnp.float32)
        at = pl.multiple_of(d * (rows_each + 2 * lines) + rows_each, 2 * SUB)
        send_ref[pl.ds(at, 2 * lines), :] = digits.astype(jnp.bfloat16)


def partials(capacity, src_count, src_rows, home_row, home_tag, recon, tgt, weight):
    columns = recon.shape[1]
    blocks = tgt.shape[0]
    lines = tag_lines(capacity)
    smem = pl.BlockSpec(memory_space=pltpu.SMEM)
    vmem = pl.BlockSpec(memory_space=pltpu.VMEM)
    return pl.pallas_call(
        functools.partial(partial_kernel, capacity, src_count),
        out_shape=jax.ShapeDtypeStruct(
            (src_count * (capacity * TB + 2 * lines), columns), jnp.bfloat16
        ),
        in_specs=[smem] * 3 + [vmem] * 3,
        out_specs=vmem,
        scratch_shapes=[
            pltpu.VMEM((UNROLL, 3 * SPAN, columns), jnp.float32),
            pltpu.VMEM((src_count * lines, LANES), jnp.int32),
        ],
        compiler_params=pltpu.CompilerParams(vmem_limit_bytes=24 << 20),
        cost_estimate=pl.CostEstimate(
            flops=8 * blocks * SB * 3 * TB * columns,
            bytes_accessed=60_000_000,
            transcendentals=0,
        ),
        name="partials",
    )(src_rows, home_row, home_tag, recon, tgt, weight)


def exchange_kernel(
    count, level_count, lev_count, rows, level_ref, send_ref,
    remapped_ref, sum_ref,
    far_in, near_in, total, dense_out, dense_in, local_sum, other_sum,
    out_sem, in_sem, dense_sem, sum_sem,
):
    half = count // 2
    me = lax.axis_index("src")
    lev = lax.axis_index("lev")
    group = (me // half) * half
    place = me - group
    mirror = lax.rem(me + half, count)
    partner = lax.rem(lev + 1, lev_count)
    targets, columns = total.shape
    step = min(LANES, rows)
    lines = rows // step

    def peer(t):
        return group + lax.rem(place + t, half)

    barrier = pltpu.get_barrier_semaphore()

    @pl.loop(1, half)
    def _(t):
        pl.semaphore_signal(barrier, inc=1, device_id=(peer(t), lev), device_id_type=MESH)

    pl.semaphore_signal(barrier, inc=1, device_id=(mirror, lev), device_id_type=MESH)
    pl.semaphore_signal(barrier, inc=1, device_id=(me, partner), device_id_type=MESH)
    pl.semaphore_wait(barrier, half + 1)

    def copy(kind, t):
        to = peer(t)
        owner = lax.rem(to + half, count) if kind == 0 else to
        return pltpu.make_async_remote_copy(
            src_ref=send_ref.at[owner], dst_ref=(far_in, near_in)[kind].at[t],
            send_sem=out_sem.at[kind, t], recv_sem=in_sem.at[kind, t],
            device_id=(to, lev), device_id_type=MESH,
        )

    for kind in range(2):

        @pl.loop(1, half)
        def _(t, kind=kind):
            copy(kind, t).start()

    def add(chunk):
        digits = chunk[rows:, :].astype(jnp.float32)
        lead = digits.shape[0] // 2
        cell = (digits[:lead] * 256.0 + digits[lead:]).astype(jnp.int32)
        where = lax.broadcasted_iota(jnp.int32, (targets, step), 0)
        hits = [
            jnp.where(where == cell[m:m + 1, :step], 1.0, 0.0).astype(jnp.bfloat16)
            for m in range(lines)
        ]
        hits = hits[0] if lines == 1 else jnp.concatenate(hits, axis=1)
        total[...] += jnp.dot(hits, chunk[:rows, :], preferred_element_type=jnp.float32)

    total[...] = jnp.zeros_like(total)
    add(send_ref[mirror])

    @pl.loop(1, half)
    def _(t):
        copy(0, t).wait_recv()
        add(far_in[t])

    dense_out[...] = total[...].astype(jnp.bfloat16)
    dense = pltpu.make_async_remote_copy(
        src_ref=dense_out, dst_ref=dense_in, send_sem=dense_sem.at[0], recv_sem=dense_sem.at[1],
        device_id=(mirror, lev), device_id_type=MESH,
    )
    dense.start()
    total[...] = jnp.zeros_like(total)
    add(send_ref[me])

    @pl.loop(1, half)
    def _(t):
        copy(1, t).wait_recv()
        add(near_in[t])

    dense.wait_recv()
    result = total[...] + dense_in[...].astype(jnp.float32)
    remapped_ref[...] = result.astype(jnp.bfloat16)
    start = lev * level_count
    which = lax.broadcasted_iota(jnp.int32, (FIELDS, columns), 1)
    line = lax.broadcasted_iota(jnp.int32, (FIELDS, columns), 0)
    mix = jnp.zeros((FIELDS, columns), jnp.float32)
    for l in range(level_count):
        mix = jnp.where(which == line + l * FIELDS, level_ref[start + l], mix)
    local_sum[...] = lax.dot_general(
        mix,
        result,
        (((1,), (1,)), ((), ())),
        precision=lax.Precision.HIGHEST,
        preferred_element_type=jnp.float32,
    )
    swap = pltpu.make_async_remote_copy(
        src_ref=local_sum, dst_ref=other_sum, send_sem=sum_sem.at[0], recv_sem=sum_sem.at[1],
        device_id=(me, partner), device_id_type=MESH,
    )
    swap.start()

    @pl.loop(1, half)
    def _(t):
        copy(0, t).wait_send()
        copy(1, t).wait_send()

    dense.wait_send()
    swap.wait()
    sum_ref[...] = local_sum[...] + other_sum[...]


def exchange(level_weight, sent, rows, count, lev_count, level_count):
    columns = sent.shape[2]
    half = count // 2
    smem = pl.BlockSpec(memory_space=pltpu.SMEM)
    vmem = pl.BlockSpec(memory_space=pltpu.VMEM)
    landing = pltpu.VMEM((half,) + sent.shape[1:], jnp.bfloat16)
    return pl.pallas_call(
        functools.partial(exchange_kernel, count, level_count, lev_count, rows),
        out_shape=(
            jax.ShapeDtypeStruct((T_DEV, columns), jnp.bfloat16),
            jax.ShapeDtypeStruct((FIELDS, T_DEV), jnp.float32),
        ),
        in_specs=[smem, vmem],
        out_specs=(vmem, vmem),
        scratch_shapes=[
            landing,
            landing,
            pltpu.VMEM((T_DEV, columns), jnp.float32),
            pltpu.VMEM((T_DEV, columns), jnp.bfloat16),
            pltpu.VMEM((T_DEV, columns), jnp.bfloat16),
            pltpu.VMEM((FIELDS, T_DEV), jnp.float32),
            pltpu.VMEM((FIELDS, T_DEV), jnp.float32),
            pltpu.SemaphoreType.DMA((2, half)),
            pltpu.SemaphoreType.DMA((2, half)),
            pltpu.SemaphoreType.DMA((2,)),
            pltpu.SemaphoreType.DMA((2,)),
        ],
        compiler_params=pltpu.CompilerParams(
            vmem_limit_bytes=40 << 20, collective_id=0, has_side_effects=True
        ),
        name="exchange",
    )(level_weight, sent)


def shards(field, grad_coef, neighbours, level_weight, src_index, tgt_index, block_dest, weights):
    src_count = lax.axis_size("src")
    columns = field.shape[1]
    blocks = src_index.shape[0]
    capacity = 2 * blocks // src_count
    owner = block_dest[:, 0]
    order = jnp.arange(blocks, dtype=jnp.int32)
    earlier = (owner[:, None] == owner[None, :]) & (order[:, None] < order[None, :])
    rank = jnp.sum(earlier.astype(jnp.int32), axis=0)
    lines = tag_lines(capacity)
    home_row = owner * (capacity * TB + 2 * lines) + rank * TB
    home_tag = owner * (lines * GROUP) + rank
    shaped = weights.reshape(blocks, 3 * SB * TB // LANES, LANES)
    sent = partials(
        capacity, src_count, src_index * SUB, home_row, home_tag,
        prepare(src_count, field, grad_coef, neighbours.T), jnp.tile(tgt_index, (1, GROUP)), shaped,
    )
    return exchange(
        level_weight, sent.reshape(src_count, -1, columns), capacity * TB, src_count, lax.axis_size("lev"), columns // FIELDS
    )


def solution(mesh):
    placed = (
        P("src", "lev"),
        P(None, None, "src"),
        P("src", None),
        P(),
        P("src", None),
        P("src", None),
        P("src", None),
        P("src", None),
    )
    return jax.shard_map(
        shards,
        mesh=mesh,
        in_specs=placed,
        out_specs=(P("src", "lev"), P(None, "src")),
        check_vma=False,
    )
```

profile of v0, /device:TPU:15, one launch (start us, length us, event | category | flops | bytes accessed | tf_op | source)
XLA Modules:
  0.0 69.5 jit_solution(2908278349341311185)
XLA Ops:
  0.6 0.0 copy-start.2
  0.6 0.0 copy-start.1
  0.6 0.0 copy-start
  0.7 0.8 %convert_reduce_fusion = s32[128]{0:T(128)S(1)} fusion(s32[128]{0:T(128)} %bitcast.13), kind=kLoop, calls=%fused_computation | loop fusion | flops 81792 | bytes 1024 | tf_op jit(solution)/shard_map/reduce_sum | solution.py:360
  1.5 0.7 multiply_add_fusion
  2.2 0.8 %copy.16 = s32[128,64]{1,0:T(8,128)S(1)} copy(s32[128,64]{0,1:T(8,128)} %param.12) | data formatting | bytes 65536 | tf_op args[4]
  3.0 0.7 %tile.4 = s32[128,4,32]{0,2,1:T(8,128)S(1)} broadcast(s32[128,32]{0,1:T(8,128)} %param.13), dimensions={0,2} | broadcast | bytes 81920 | tf_op jit(solution)/shard_map/tile | solution.py:367
  3.7 0.1 copy.18.tgt_ref
  3.8 1.8 %copy.19 = bf16[16,8,48,128]{3,2,1,0:T(8,128)(2,1)S(1)} copy(bf16[16,8,48,128]{3,1,2,0:T(8,128)(2,1)} %bitcast.11) | data formatting | bytes 3145728
  5.6 0.0 copy-done.2
  5.6 0.0 copy-done.1
  5.6 0.0 copy-done
  5.6 6.9 %prepare.1.recon = f32[16384,128]{1,0:T(8,128)S(1)} custom-call(bf16[2048,128]{1,0:T(8,128)(2,1)S(1)} %copy-done, f32[2,4,2048]{2,1,0:T(4,128)S(1)} %copy-done.1, s32[4,2048]{1,0:T(4,128)S(1)} %bitcast.10), custom_call_target="tpu_custom_call" | custom-call | tf_op jit(solution)/shard_map/prepare/pallas_call | solution.py:109
  12.6 0.0 copy-start.3
  12.6 15.1 %partials.1 = bf16[8448,128]{1,0:T(8,128)(2,1)S(1)} custom-call(s32[128,64]{1,0:T(8,128)S(1)} %broadcast_multiply_fusion.src_ref, s32[128]{0:T(128)S(1)} %get-tuple-element.3.row_ref, s32[128]{0:T(128)S(1)} %get-tuple-element.2.tag_ref, f32[16384,128]{1,0:T(8,128)S(1)} %prepare.1.recon, s32[128,128]{1,0:T(8,128)S(1)} %copy.18.tgt_ref, ...), custom_call_target="tpu_custom_call" | custom-call | flops 805306368 | bytes 60000000 | tf_op jit(solution)/shard_map/partials/pallas_call | solution.py:186
  27.7 0.0 copy-done.3
  27.7 40.4 %exchange.1 = (bf16[1024,128]{1,0:T(8,128)(2,1)S(1)}, f32[32,1024]{1,0:T(8,128)S(1)}) custom-call(f32[8]{0:T(128)S(1)} %copy-done.3, bf16[16,528,128]{2,1,0:T(8,128)(2,1)S(1)} %bitcast.8), custom_call_target="tpu_custom_call" | custom-call | tf_op jit(solution)/shard_map/exchange/pallas_call | solution.py:324
  68.2 0.7 %copy.22 = bf16[1024,128]{1,0:T(8,128)(2,1)} copy(bf16[1024,128]{1,0:T(8,128)(2,1)S(1)} %get-tuple-element.6) | data formatting | bytes 524288
  68.9 0.7 copy.23
  (1 shorter events, 0.0 us)
Async XLA Ops:
  0.6 5.0 %copy-start.2 = (s32[2048,4]{0,1:T(4,128)S(1)}, s32[2048,4]{0,1:T(4,128)}, u32[]{:S(2)}) copy-start(s32[2048,4]{0,1:T(4,128)} %param.10) | copy-start | bytes 98308
  0.6 5.0 %copy-start.1 = (f32[2,4,2048]{2,1,0:T(4,128)S(1)}, f32[2,4,2048]{2,1,0:T(4,128)}, u32[]{:S(2)}) copy-start(f32[2,4,2048]{2,1,0:T(4,128)} %coef_ref.1) | copy-start | bytes 196612
  0.6 5.0 %copy-start = (bf16[2048,128]{1,0:T(8,128)(2,1)S(1)}, bf16[2048,128]{1,0:T(8,128)(2,1)}, u32[]{:S(2)}) copy-start(bf16[2048,128]{1,0:T(8,128)(2,1)} %field_ref.1) | copy-start | bytes 1572868
  12.6 15.1 %copy-start.3 = (f32[8]{0:T(128)S(1)}, f32[8]{0:T(128)}, u32[]{:S(2)}) copy-start(f32[8]{0:T(128)} %level_ref.1) | copy-start | bytes 100
where the time goes:
time: 69.9 us; the launch traced here: 69.5 us
  Pallas kernels  62.5 us (89%)
  local copies, waits for them, and re-layouts  4.8 us (7%)
  other arithmetic  1.5 us (2%)
  between operations  0.75 us (1%)
    pallas_call x1, Pallas kernels, exchange(): pl.pallas_call(functools.partial(exchange_kernel, count, level_count, lev...  40.4 us
    pallas_call x1, Pallas kernels, partials(): pl.pallas_call(functools.partial(partial_kernel, capacity, src_count), ou...  15.1 us
    pallas_call x1, Pallas kernels, prepare(): pl.pallas_call(functools.partial(prepare_kernel, count), out_shape=jax.Sh...  6.94 us
    unnamed x12, local copies, waits for them, and re-layouts  3.98 us

commit v1 on v0

v1 whole, which is shorter than its diff:
```python
import functools

import jax
import jax.numpy as jnp
from jax import lax
from jax.experimental import pallas as pl
from jax.experimental.pallas import tpu as pltpu
from jax.sharding import PartitionSpec as P

FIELDS = 32
HW = 64
SB = 64
TB = 32
T_DEV = 1024
LANES = 128
SUB = 8
TILE = 128
GROUP = LANES // TB
GROUP_BITS = GROUP.bit_length() - 1
PIECE = 32
UNROLL = 4
BATCH = 16
SPAN = SB + SUB
PLANE = 4
PAIR = 2
BAND = 256
MESH = pl.DeviceIdType.MESH


def contract_first(a, b):
    return lax.dot_general(a, b, (((0,), (0,)), ((), ())), preferred_element_type=jnp.float32)


def contract_last(a, b):
    return lax.dot_general(a, b, (((1,), (1,)), ((), ())), preferred_element_type=jnp.float32)


def place(count):
    me = lax.axis_index("src")
    column = PLANE * PAIR
    return me // column, lax.rem(me // PLANE, PAIR), lax.rem(me, PLANE), count // column


def one_hot(mask):
    return jnp.where(mask, 1.0, 0.0).astype(jnp.bfloat16)


def plan(count, dest_ref, tgt_ref, src_ref, order_ref, start_ref, tags_ref, cells_ref):
    blocks = dest_ref.shape[1]
    outer, inner, plane, outers = place(count)
    steps = count // PLANE
    owner = dest_ref[...]
    turn = lax.shift_right_logical(owner, 3) - outer - 1
    turn = jnp.where(turn < 0, turn + outers, turn)
    same = jnp.bitwise_and(lax.shift_right_logical(owner, 2), 1) == inner
    step = 2 * turn + jnp.where(same, 1, 0)
    apart = jnp.bitwise_xor(jnp.bitwise_and(owner, PLANE - 1), plane)
    spot = jnp.where(apart == 3, 0, jnp.where(apart == 0, 3, apart))
    key = step * PLANE + spot
    slots = spot * steps + step

    keys = max(count, LANES)
    rows = lax.broadcasted_iota(jnp.int32, (keys, blocks), 0)
    hit = rows == key
    ones = one_hot(hit)
    before = one_hot(
        lax.broadcasted_iota(jnp.int32, (blocks, blocks), 0)
        < lax.broadcasted_iota(jnp.int32, (blocks, blocks), 1)
    )
    less = one_hot(
        lax.broadcasted_iota(jnp.int32, (keys, keys), 1)
        < lax.broadcasted_iota(jnp.int32, (keys, keys), 0)
    )
    prefix = jnp.dot(ones, before, preferred_element_type=jnp.float32)
    ahead = jnp.dot(less, ones, preferred_element_type=jnp.float32)
    starts = jnp.sum(ahead, axis=1, keepdims=True)
    rank = jnp.sum(jnp.where(hit, prefix, 0.0), axis=0, keepdims=True).astype(jnp.int32)
    at = rank + jnp.sum(jnp.where(hit, starts, 0.0), axis=0, keepdims=True).astype(jnp.int32)
    start_ref[...] = contract_last(
        jnp.ones((SUB, blocks), jnp.bfloat16), ahead.astype(jnp.bfloat16)
    ).astype(jnp.int32)
    here = one_hot(lax.broadcasted_iota(jnp.int32, (blocks, blocks), 0) == at)
    names = lax.broadcasted_iota(jnp.int32, (SUB, blocks), 1).astype(jnp.float32)
    order_ref[...] = contract_last(names.astype(jnp.bfloat16), here).astype(jnp.int32)
    source = src_ref[...]
    digits = [lax.shift_right_logical(source, 5), jnp.bitwise_and(source, 31)]
    moved = [contract_last(d.astype(jnp.float32).astype(jnp.bfloat16), here) for d in digits]
    cells_ref[...] = (moved[0] * 32.0 + moved[1]).astype(jnp.int32)

    line = slots * SUB + lax.shift_right_logical(rank, GROUP_BITS)
    lane = jnp.bitwise_and(rank, GROUP - 1)
    cell = tgt_ref[...] + 1
    high = lax.shift_right_logical(cell, 5).astype(jnp.float32)
    low = jnp.bitwise_and(cell, 31).astype(jnp.float32)
    found = [None, None]
    lines = lax.broadcasted_iota(jnp.int32, (count * SUB, blocks), 0) == line
    group = lax.broadcasted_iota(jnp.int32, (LANES, blocks), 0) // TB
    for q in range(GROUP):
        mine = one_hot(jnp.logical_and(lines, lane == q))
        for g, digit in enumerate((high, low)):
            spread = jnp.where(group == q, jnp.concatenate([digit] * GROUP, axis=0), 0.0)
            part = contract_last(mine, spread.astype(jnp.bfloat16))
            found[g] = part if found[g] is None else found[g] + part
    tags_ref[...] = (found[0] * 32.0 + found[1]).astype(jnp.int32) - 1


def prepare_kernel(
    count, field_ref, coef_ref, near_ref, dest_ref, tgt_ref, src_ref,
    recon, order_ref, start_ref, tags_ref, cells_ref,
    ext, mixes, out_sem, in_sem,
):
    cells = field_ref.shape[0]
    window = TILE + 2 * HW
    tiles = cells // TILE
    me = lax.axis_index("src")
    lev = lax.axis_index("lev")
    right = lax.rem(me + 1, count)
    left = lax.rem(me + count - 1, count)
    barrier = pltpu.get_barrier_semaphore()
    for other in (left, right):
        pl.semaphore_signal(barrier, inc=1, device_id=(other, lev), device_id_type=MESH)
    ext[HW:HW + cells, :] = field_ref[...]
    plan(count, dest_ref, tgt_ref, src_ref, order_ref, start_ref, tags_ref, cells_ref)

    def tile(t):
        base = pl.multiple_of(t * TILE, TILE)
        near = near_ref[:, pl.ds(base, TILE)] - base
        coef = [coef_ref[g, :, pl.ds(base, TILE)] for g in range(2)]
        totals = [-jnp.sum(coef[g], axis=0, keepdims=True) for g in range(2)]
        held = ext[pl.ds(base, window), :]
        rows = pl.multiple_of(base * SUB, TILE * SUB)
        recon[pl.ds(rows, TILE, stride=SUB), :] = field_ref[pl.ds(base, TILE), :].astype(
            jnp.float32
        )
        for w in range(0, window, PIECE):
            here = lax.broadcasted_iota(jnp.int32, (PIECE, TILE), 0) + w
            own = here == lax.broadcasted_iota(jnp.int32, (PIECE, TILE), 1) + HW
            mixed = [jnp.where(own, totals[g], 0.0) for g in range(2)]
            for k in range(near.shape[0]):
                hit = here == near[k:k + 1, :]
                for g in range(2):
                    mixed[g] = mixed[g] + jnp.where(hit, coef[g][k:k + 1, :], 0.0)
            for g in range(2):
                high = mixed[g].astype(jnp.bfloat16)
                rest = (mixed[g] - high.astype(jnp.float32)).astype(jnp.bfloat16)
                mixes[w:w + PIECE, 2 * g * TILE:(2 * g + 1) * TILE] = high
                mixes[w:w + PIECE, (2 * g + 1) * TILE:(2 * g + 2) * TILE] = rest
        for g in range(2):
            value = contract_first(mixes[:, 2 * g * TILE:(2 * g + 1) * TILE], held)
            value = value + contract_first(mixes[:, (2 * g + 1) * TILE:(2 * g + 2) * TILE], held)
            recon[pl.ds(rows + 1 + g, TILE, stride=SUB), :] = value

    @pl.loop(1, tiles // 2)
    def _(t):
        tile(t)

    pl.semaphore_wait(barrier, 2)
    low = pltpu.make_async_remote_copy(
        src_ref=field_ref.at[pl.ds(cells - HW, HW)], dst_ref=ext.at[pl.ds(0, HW)],
        send_sem=out_sem.at[0], recv_sem=in_sem.at[0],
        device_id=(right, lev), device_id_type=MESH,
    )
    high = pltpu.make_async_remote_copy(
        src_ref=field_ref.at[pl.ds(0, HW)], dst_ref=ext.at[pl.ds(HW + cells, HW)],
        send_sem=out_sem.at[1], recv_sem=in_sem.at[1],
        device_id=(left, lev), device_id_type=MESH,
    )
    low.start()
    high.start()

    @pl.loop(tiles // 2, tiles - 1)
    def _(t):
        tile(t)

    low.wait()
    high.wait()

    @pl.loop(0, 2)
    def _(e):
        tile(e * (tiles - 1))


def prepare(count, field, coef, near_t, dest_t, tgt_t, src_t):
    cells, columns = field.shape
    vmem = pl.BlockSpec(memory_space=pltpu.VMEM)
    return pl.pallas_call(
        functools.partial(prepare_kernel, count),
        out_shape=(
            jax.ShapeDtypeStruct((cells * SUB, columns), jnp.float32),
            jax.ShapeDtypeStruct((SUB, dest_t.shape[1]), jnp.int32),
            jax.ShapeDtypeStruct((SUB, max(count, LANES)), jnp.int32),
            jax.ShapeDtypeStruct((count * SUB, LANES), jnp.int32),
            jax.ShapeDtypeStruct(src_t.shape, jnp.int32),
        ),
        in_specs=[vmem] * 6,
        out_specs=(vmem,) * 5,
        scratch_shapes=[
            pltpu.VMEM((cells + 2 * HW, columns), jnp.bfloat16),
            pltpu.VMEM((TILE + 2 * HW, 4 * TILE), jnp.bfloat16),
            pltpu.SemaphoreType.DMA((2,)),
            pltpu.SemaphoreType.DMA((2,)),
        ],
        compiler_params=pltpu.CompilerParams(
            vmem_limit_bytes=24 << 20, collective_id=1, has_side_effects=True
        ),
        name="prepare",
    )(field, coef, near_t, dest_t, tgt_t, src_t)


def remap_kernel(
    count, capacity, level_count, lev_count,
    src_ref, order_ref, start_ref, level_ref, recon, weight_ref, tags_ref,
    remapped_ref, sum_ref,
    picked, compact, staged, land, seen, total, dense_out, dense_in, local_sum, other_sum,
    chunk_out, chunk_in, tag_out, tag_in, line_out, line_in, sum_sem,
):
    me = lax.axis_index("src")
    lev = lax.axis_index("lev")
    outer, inner, plane, outers = place(count)
    steps = count // PLANE
    base = me - plane
    rows = capacity * TB
    width = min(LANES, rows)
    lines = rows // width
    targets, columns = total.shape
    partner_lev = lax.rem(lev + 1, lev_count)
    peers = [
        base + PLANE - 1 - plane,
        base + plane + 1 - 2 * lax.rem(plane, 2),
        base + lax.rem(plane + 2, PLANE),
    ]
    partner = me + PLANE * (1 - 2 * inner)

    def mirror(turn):
        return lax.rem(outer + turn, outers) * PLANE * PAIR + inner * PLANE + plane

    barrier = pltpu.get_barrier_semaphore()
    for other in peers + [partner]:
        pl.semaphore_signal(barrier, inc=1, device_id=(other, lev), device_id_type=MESH)

    @pl.loop(1, outers)
    def _(t):
        pl.semaphore_signal(barrier, inc=1, device_id=(mirror(t), lev), device_id_type=MESH)

    pl.semaphore_signal(barrier, inc=1, device_id=(me, partner_lev), device_id_type=MESH)

    @pl.loop(0, compact.shape[0] // SUB)
    def _(n):
        compact[pl.ds(n * SUB, SUB)] = jnp.zeros((SUB, TB, columns), jnp.bfloat16)

    seen[PLANE - 1] = tags_ref[PLANE - 1]
    pl.semaphore_wait(barrier, PLANE + outers)

    def tag_copy(spot):
        return pltpu.make_async_remote_copy(
            src_ref=tags_ref.at[spot], dst_ref=seen.at[spot],
            send_sem=tag_out.at[spot], recv_sem=tag_in.at[spot],
            device_id=(peers[spot], lev), device_id_type=MESH,
        )

    def chunk_copy(step, spot):
        return pltpu.make_async_remote_copy(
            src_ref=staged.at[step, spot], dst_ref=land.at[step, spot],
            send_sem=chunk_out.at[step, spot], recv_sem=chunk_in.at[step, spot],
            device_id=(peers[spot], lev), device_id_type=MESH,
        )

    def line_copy(step, to):
        return pltpu.make_async_remote_copy(
            src_ref=dense_out.at[step], dst_ref=dense_in.at[step],
            send_sem=line_out.at[step], recv_sem=line_in.at[step],
            device_id=(to, lev), device_id_type=MESH,
        )

    for spot in range(PLANE - 1):
        tag_copy(spot).start()

    def one(i, buffer):
        for begin in range(0, SB, BATCH):
            found = [recon[src_ref[begin + j, i]] for j in range(BATCH)]
            for j in range(BATCH):
                to = ((begin + j) % GROUP) * (SB // GROUP) + (begin + j) // GROUP
                buffer[pl.ds(to, 3, stride=SPAN), :] = found[j][0:3, :]
        held = weight_ref[order_ref[0, i]]
        whole = None
        for q in range(GROUP):
            parts = [
                buffer[pl.ds(c * SPAN + q * (SB // GROUP), SB // GROUP), :] for c in range(3)
            ]
            terms = jnp.concatenate(parts, axis=0).astype(jnp.bfloat16)
            product = contract_first(held[:, q * TB:(q + 1) * TB], terms)
            whole = product if whole is None else whole + product
        compact[i] = whole.astype(jnp.bfloat16)

    def stage(step, spot):
        chunk = compact[pl.ds(start_ref[0, step * PLANE + spot], capacity)].reshape(rows, columns)
        if spot < PLANE - 1:
            staged[step, spot] = chunk
            chunk_copy(step, spot).start()
        else:
            land[step, spot] = chunk

    unroll = min(UNROLL, capacity)

    @pl.loop(0, steps // 2)
    def _(step):
        for spot in range(PLANE):

            @pl.loop(0, capacity // unroll)
            def _(n, spot=spot):
                first = (step * PLANE + spot) * capacity + n * unroll
                for m in range(unroll):
                    one(first + m, picked.at[m])

            stage(step, spot)

    @pl.loop(steps // 2, steps)
    def _(step):
        for spot in range(PLANE):
            stage(step, spot)

    for spot in range(PLANE - 1):
        tag_copy(spot).wait_recv()

    def add(step, spot, fresh):
        cell = seen[spot, step]
        part = lax.shift_right_arithmetic(cell, 8)
        low = jnp.bitwise_and(cell, BAND - 1)
        chunk = land[step, spot]
        where = lax.broadcasted_iota(jnp.int32, (BAND, width), 0).astype(jnp.float32)
        where = where.astype(jnp.bfloat16)
        for h in range(targets // BAND):
            mark = jnp.where(part == h, low, -1).astype(jnp.float32).astype(jnp.bfloat16)
            hits = [
                jnp.where(where == mark[m:m + 1, :width], 1.0, 0.0).astype(jnp.bfloat16)
                for m in range(lines)
            ]
            hits = hits[0] if lines == 1 else jnp.concatenate(hits, axis=1)
            sums = jnp.dot(hits, chunk, preferred_element_type=jnp.float32)
            band = pl.ds(h * BAND, BAND)
            total[band, :] = sums if fresh else total[band, :] + sums

    def gather(step):
        add(step, PLANE - 1, True)
        for spot in range(PLANE - 1):

            def ready(spot=spot):
                chunk_copy(step, spot).wait_recv()

            ready()
            add(step, spot, False)

    def near(step):
        gather(step)
        dense_out[step] = total[...].astype(jnp.bfloat16)
        line_copy(step, partner).start()

    @pl.loop(0, outers - 1)
    def _(turn):
        step = 2 * turn
        near(step)
        gather(step + 1)
        line_copy(step, partner).wait_recv()
        both = total[...] + dense_in[step].astype(jnp.float32)
        dense_out[step + 1] = both.astype(jnp.bfloat16)
        line_copy(step + 1, mirror(turn + 1)).start()

    near(steps - 2)
    gather(steps - 1)
    line_copy(steps - 2, partner).wait_recv()
    total[...] += dense_in[steps - 2].astype(jnp.float32)

    @pl.loop(0, outers - 1)
    def _(turn):
        line_copy(2 * turn + 1, mirror(turn + 1)).wait_recv()
        total[...] += dense_in[2 * turn + 1].astype(jnp.float32)

    result = total[...]
    remapped_ref[...] = result.astype(jnp.bfloat16)
    start = lev * level_count
    which = lax.broadcasted_iota(jnp.int32, (FIELDS, columns), 1)
    line = lax.broadcasted_iota(jnp.int32, (FIELDS, columns), 0)
    mix = jnp.zeros((FIELDS, columns), jnp.float32)
    for l in range(level_count):
        mix = jnp.where(which == line + l * FIELDS, level_ref[start + l], mix)
    local_sum[...] = lax.dot_general(
        mix,
        result,
        (((1,), (1,)), ((), ())),
        precision=lax.Precision.HIGHEST,
        preferred_element_type=jnp.float32,
    )
    swap = pltpu.make_async_remote_copy(
        src_ref=local_sum, dst_ref=other_sum, send_sem=sum_sem.at[0], recv_sem=sum_sem.at[1],
        device_id=(me, partner_lev), device_id_type=MESH,
    )
    swap.start()
    for spot in range(PLANE - 1):
        tag_copy(spot).wait_send()

    @pl.loop(0, steps)
    def _(step):
        for spot in range(PLANE - 1):
            chunk_copy(step, spot).wait_send()

    @pl.loop(0, steps - 1)
    def _(step):
        line_copy(step, partner).wait_send()

    swap.wait()
    sum_ref[...] = local_sum[...] + other_sum[...]


def remap(count, capacity, lev_count, level_count, src_t, order, start, level, recon, weight, tags):
    columns = recon.shape[2]
    blocks = src_t.shape[1]
    steps = count // PLANE
    rows = capacity * TB
    smem = pl.BlockSpec(memory_space=pltpu.SMEM)
    vmem = pl.BlockSpec(memory_space=pltpu.VMEM)
    dma = pltpu.SemaphoreType.DMA
    chunk = (rows, columns)
    dense = (T_DEV, columns)
    return pl.pallas_call(
        functools.partial(remap_kernel, count, capacity, level_count, lev_count),
        out_shape=(
            jax.ShapeDtypeStruct(dense, jnp.bfloat16),
            jax.ShapeDtypeStruct((FIELDS, T_DEV), jnp.float32),
        ),
        in_specs=[smem] * 4 + [vmem] * 3,
        out_specs=(vmem, vmem),
        scratch_shapes=[
            pltpu.VMEM((UNROLL, 3 * SPAN, columns), jnp.float32),
            pltpu.VMEM((-(-(blocks + capacity) // SUB) * SUB, TB, columns), jnp.bfloat16),
            pltpu.VMEM((steps, PLANE - 1) + chunk, jnp.bfloat16),
            pltpu.VMEM((steps, PLANE) + chunk, jnp.bfloat16),
            pltpu.VMEM((PLANE, steps, SUB, LANES), jnp.int32),
            pltpu.VMEM(dense, jnp.float32),
            pltpu.VMEM((steps - 1,) + dense, jnp.bfloat16),
            pltpu.VMEM((steps - 1,) + dense, jnp.bfloat16),
            pltpu.VMEM((FIELDS, T_DEV), jnp.float32),
            pltpu.VMEM((FIELDS, T_DEV), jnp.float32),
            dma((steps, PLANE - 1)),
            dma((steps, PLANE - 1)),
            dma((PLANE - 1,)),
            dma((PLANE - 1,)),
            dma((steps - 1,)),
            dma((steps - 1,)),
            dma((2,)),
        ],
        compiler_params=pltpu.CompilerParams(
            vmem_limit_bytes=52 << 20, collective_id=0, has_side_effects=True
        ),
        name="remap",
    )(src_t, order, start, level, recon, weight, tags)


def shards(field, grad_coef, neighbours, level_weight, src_index, tgt_index, block_dest, weights):
    count = lax.axis_size("src")
    columns = field.shape[1]
    blocks = src_index.shape[0]
    capacity = 2 * blocks // count
    steps = count // PLANE
    shaped = weights.reshape(blocks, 3 * SB * TB // LANES, LANES)
    recon, order, start, tags, cells = prepare(
        count, field, grad_coef, neighbours.T, block_dest.T, tgt_index.T, src_index.T
    )
    return remap(
        count, capacity, lax.axis_size("lev"), columns // FIELDS, cells, order, start,
        level_weight, recon.reshape(-1, SUB, columns), shaped, tags.reshape(PLANE, steps, SUB, LANES),
    )


def solution(mesh):
    placed = (
        P("src", "lev"),
        P(None, None, "src"),
        P("src", None),
        P(),
        P("src", None),
        P("src", None),
        P("src", None),
        P("src", None),
    )
    return jax.shard_map(
        shards,
        mesh=mesh,
        in_specs=placed,
        out_specs=(P("src", "lev"), P(None, "src")),
        check_vma=False,
    )
```

time: 69.9 us -> 70.2 us (level)
  the two profiles are of different devices: /device:TPU:15 before, /device:TPU:0 now
where the time goes in v1:
time: 70.2 us; the launch traced here: 70 us
  Pallas kernels  61.6 us (88%)
  local copies, waits for them, and re-layouts  7.62 us (11%)
  between operations  0.74 us (1%)
    pallas_call x1, Pallas kernels, remap(): pl.pallas_call(functools.partial(remap_kernel, count, capacity, level_cou...  48.5 us
    pallas_call x1, Pallas kernels, prepare(): pl.pallas_call(functools.partial(prepare_kernel, count), out_shape=(jax.S...  13.2 us
    unnamed x19, local copies, waits for them, and re-layouts  7.62 us

profile of v1, /device:TPU:0, one launch (start us, length us, event | category | flops | bytes accessed | tf_op | source)
XLA Modules:
  0.0 70.0 jit_solution(10428788128136018326)
XLA Ops:
  0.6 0.0 copy-start.1
  0.6 0.0 copy-start.2
  0.7 0.0 copy-start.3
  0.7 0.0 copy-start.4
  0.7 0.0 copy-start.5
  0.7 0.0 copy-start.6
  0.7 0.0 copy-start.7
  0.7 3.0 %copy.10 = bf16[16,8,48,128]{3,2,1,0:T(8,128)(2,1)} copy(bf16[16,8,48,128]{3,1,2,0:T(8,128)(2,1)} %bitcast.15) | data formatting | bytes 3145728
  3.7 0.0 copy-done.1
  3.7 0.0 copy-done.2
  3.7 0.0 copy-done.3
  3.7 0.0 copy-done.4
  3.7 0.0 copy-done.5
  3.7 0.0 copy-done.6
  3.8 13.2 %prepare.1 = (f32[16384,128]{1,0:T(8,128)S(1)}, s32[8,128]{1,0:T(8,128)S(1)}, s32[8,128]{1,0:T(8,128)S(1)}, s32[128,128]{1,0:T(8,128)S(1)}, s32[64,128]{1,0:T(8,128)S(1)}) custom-call(bf16[2048,128]{1,0:T(8,128)(2,1)S(1)} %copy-done.1, f32[2,4,2048]{2,1,0:T(4,128)S(1)} %copy-done.2, s32[4,2048]{1,0:T(4,128)S(1)} %bitcast.10, s32[1,128]{1,0:T(1,128)S(1)} %bitcast.13, ...), custom_call_target="tpu_custom_call" | custom-call | tf_op jit(solution)/shard_map/prepare/pallas_call | solution.py:186
  16.9 0.0 copy-start
  16.9 3.2 %copy-done = f32[16384,128]{1,0:T(8,128)} copy-done((f32[16384,128]{1,0:T(8,128)}, f32[16384,128]{1,0:T(8,128)S(1)}, u32[]{:S(2)}) %copy-start) | copy-done | bytes 8388632
  20.2 0.0 copy-done.7
  20.2 48.5 %remap.1 = (bf16[1024,128]{1,0:T(8,128)(2,1)S(1)}, f32[32,1024]{1,0:T(8,128)S(1)}) custom-call(s32[64,128]{1,0:T(8,128)S(1)} %get-tuple-element.7.src_ref, s32[8,128]{1,0:T(8,128)S(1)} %get-tuple-element.8.order_ref, s32[8,128]{1,0:T(8,128)S(1)} %get-tuple-element.9.start_ref, f32[8]{0:T(128)S(1)} %copy-done.7, f32[2048,8,128]{2,1,0:T(8,128)} %bitcast.8, ...), custom_call_target="tpu_custom_call" | custom-call | tf_op jit(solution)/shard_map/remap/pallas_call | solution.py:424
  68.6 0.7 %copy.13 = bf16[1024,128]{1,0:T(8,128)(2,1)} copy(bf16[1024,128]{1,0:T(8,128)(2,1)S(1)} %get-tuple-element.14) | data formatting | bytes 524288
  69.3 0.7 copy.14
Async XLA Ops:
  0.6 3.1 %copy-start.1 = (bf16[2048,128]{1,0:T(8,128)(2,1)S(1)}, bf16[2048,128]{1,0:T(8,128)(2,1)}, u32[]{:S(2)}) copy-start(bf16[2048,128]{1,0:T(8,128)(2,1)} %field_ref.1) | copy-start | bytes 1572868
  0.6 3.1 %copy-start.2 = (f32[2,4,2048]{2,1,0:T(4,128)S(1)}, f32[2,4,2048]{2,1,0:T(4,128)}, u32[]{:S(2)}) copy-start(f32[2,4,2048]{2,1,0:T(4,128)} %coef_ref.1) | copy-start | bytes 196612
  0.7 3.1 %copy-start.3 = (s32[2048,4]{0,1:T(4,128)S(1)}, s32[2048,4]{0,1:T(4,128)}, u32[]{:S(2)}) copy-start(s32[2048,4]{0,1:T(4,128)} %param.10) | copy-start | bytes 98308
  0.7 3.1 %copy-start.4 = (s32[128,64]{0,1:T(8,128)S(1)}, s32[128,64]{0,1:T(8,128)}, u32[]{:S(2)}) copy-start(s32[128,64]{0,1:T(8,128)} %param.12) | copy-start | bytes 98308
  0.7 3.1 %copy-start.5 = (s32[128,32]{0,1:T(8,128)S(1)}, s32[128,32]{0,1:T(8,128)}, u32[]{:S(2)}) copy-start(s32[128,32]{0,1:T(8,128)} %param.13) | copy-start | bytes 49156
  0.7 3.1 %copy-start.6 = (s32[128,1]{0,1:T(1,128)S(1)}, s32[128,1]{0,1:T(1,128)}, u32[]{:S(2)}) copy-start(s32[128,1]{0,1:T(1,128)} %param.14) | copy-start | bytes 1540
  0.7 19.5 %copy-start.7 = (f32[8]{0:T(128)S(1)}, f32[8]{0:T(128)}, u32[]{:S(2)}) copy-start(f32[8]{0:T(128)} %level_ref.1) | copy-start | bytes 100
  16.9 3.2 %copy-start = (f32[16384,128]{1,0:T(8,128)}, f32[16384,128]{1,0:T(8,128)S(1)}, u32[]{:S(2)}) copy-start(f32[16384,128]{1,0:T(8,128)S(1)} %get-tuple-element.10) | copy-start | bytes 25165828

commit v2 on v1

--- a/solution.py
+++ b/solution.py
@@ -42,7 +42,7 @@
 
 
 def one_hot(mask):
-    return jnp.where(mask, 1.0, 0.0).astype(jnp.bfloat16)
+    return jnp.where(mask, jnp.bfloat16(1), jnp.bfloat16(0))
 
 
 def plan(count, dest_ref, tgt_ref, src_ref, order_ref, start_ref, tags_ref, cells_ref):
@@ -84,7 +84,7 @@
     order_ref[...] = contract_last(names.astype(jnp.bfloat16), here).astype(jnp.int32)
     source = src_ref[...]
     digits = [lax.shift_right_logical(source, 5), jnp.bitwise_and(source, 31)]
-    moved = [contract_last(d.astype(jnp.float32).astype(jnp.bfloat16), here) for d in digits]
+    moved = [contract_last(here, d.astype(jnp.float32).astype(jnp.bfloat16)) for d in digits]
     cells_ref[...] = (moved[0] * 32.0 + moved[1]).astype(jnp.int32)
 
     line = slots * SUB + lax.shift_right_logical(rank, GROUP_BITS)
@@ -190,7 +190,7 @@
             jax.ShapeDtypeStruct((SUB, dest_t.shape[1]), jnp.int32),
             jax.ShapeDtypeStruct((SUB, max(count, LANES)), jnp.int32),
             jax.ShapeDtypeStruct((count * SUB, LANES), jnp.int32),
-            jax.ShapeDtypeStruct(src_t.shape, jnp.int32),
+            jax.ShapeDtypeStruct(src_t.shape[::-1], jnp.int32),
         ),
         in_specs=[vmem] * 6,
         out_specs=(vmem,) * 5,
@@ -275,12 +275,17 @@
     for spot in range(PLANE - 1):
         tag_copy(spot).start()
 
+    def fetch(first, unroll):
+        for begin in range(0, SB, BATCH):
+            for m in range(unroll):
+                index = src_ref.at[first + m]
+                buffer = picked.at[m]
+                found = [recon[index[begin + j]] for j in range(BATCH)]
+                for j in range(BATCH):
+                    to = ((begin + j) % GROUP) * (SB // GROUP) + (begin + j) // GROUP
+                    buffer[pl.ds(to, 3, stride=SPAN), :] = found[j][0:3, :]
+
     def one(i, buffer):
-        for begin in range(0, SB, BATCH):
-            found = [recon[src_ref[begin + j, i]] for j in range(BATCH)]
-            for j in range(BATCH):
-                to = ((begin + j) % GROUP) * (SB // GROUP) + (begin + j) // GROUP
-                buffer[pl.ds(to, 3, stride=SPAN), :] = found[j][0:3, :]
         held = weight_ref[order_ref[0, i]]
         whole = None
         for q in range(GROUP):
@@ -309,6 +314,7 @@
             @pl.loop(0, capacity // unroll)
             def _(n, spot=spot):
                 first = (step * PLANE + spot) * capacity + n * unroll
+                fetch(first, unroll)
                 for m in range(unroll):
                     one(first + m, picked.at[m])
 
@@ -332,8 +338,7 @@
         for h in range(targets // BAND):
             mark = jnp.where(part == h, low, -1).astype(jnp.float32).astype(jnp.bfloat16)
             hits = [
-                jnp.where(where == mark[m:m + 1, :width], 1.0, 0.0).astype(jnp.bfloat16)
-                for m in range(lines)
+                one_hot(where == mark[m:m + 1, :width]) for m in range(lines)
             ]
             hits = hits[0] if lines == 1 else jnp.concatenate(hits, axis=1)
             sums = jnp.dot(hits, chunk, preferred_element_type=jnp.float32)
@@ -411,9 +416,9 @@
     sum_ref[...] = local_sum[...] + other_sum[...]
 
 
-def remap(count, capacity, lev_count, level_count, src_t, order, start, level, recon, weight, tags):
+def remap(count, capacity, lev_count, level_count, cells, order, start, level, recon, weight, tags):
     columns = recon.shape[2]
-    blocks = src_t.shape[1]
+    blocks = cells.shape[0]
     steps = count // PLANE
     rows = capacity * TB
     smem = pl.BlockSpec(memory_space=pltpu.SMEM)
@@ -449,10 +454,10 @@
             dma((2,)),
         ],
         compiler_params=pltpu.CompilerParams(
-            vmem_limit_bytes=52 << 20, collective_id=0, has_side_effects=True
+            vmem_limit_bytes=(12 << 20) + steps * (3 << 18), collective_id=0, has_side_effects=True
         ),
         name="remap",
-    )(src_t, order, start, level, recon, weight, tags)
+    )(cells, order, start, level, recon, weight, tags)
 
 
 def shards(field, grad_coef, neighbours, level_weight, src_index, tgt_index, block_dest, weights):

time: 70.2 us -> 59.5 us (0.85)
  Pallas kernels: 61.6 us -> 55.4 us
  local copies, waits for them, and re-layouts: 7.62 us -> 3.19 us
    pallas_call x1, Pallas kernels: 48.5 us -> 42.3 us  [remap(): pl.pallas_call(functools.partial(remap_kernel, count, capacity, level_cou...]
    unnamed x19 -> x17, local copies, waits for them, and re-layouts: 7.62 us -> 3.19 us
where the time goes in v2:
time: 59.5 us; the launch traced here: 59.4 us
  Pallas kernels  55.4 us (93%)
  local copies, waits for them, and re-layouts  3.19 us (5%)
  between operations  0.77 us (1%)
    pallas_call x1, Pallas kernels, remap(): pl.pallas_call(functools.partial(remap_kernel, count, capacity, level_cou...  42.3 us
    pallas_call x1, Pallas kernels, prepare(): pl.pallas_call(functools.partial(prepare_kernel, count), out_shape=(jax.S...  13.2 us
    unnamed x17, local copies, waits for them, and re-layouts  3.19 us

profile of v2, /device:TPU:0, one launch (start us, length us, event | category | flops | bytes accessed | tf_op | source)
XLA Modules:
  0.0 59.4 jit_solution(9658613784705789781)
XLA Ops:
  0.6 0.0 copy-start
  0.6 0.0 copy-start.1
  0.7 0.0 copy-start.2
  0.7 0.0 copy-start.3
  0.7 0.0 copy-start.4
  0.7 0.0 copy-start.5
  0.7 0.0 copy-start.6
  0.7 1.8 %copy.10 = bf16[16,8,48,128]{3,2,1,0:T(8,128)(2,1)S(1)} copy(bf16[16,8,48,128]{3,1,2,0:T(8,128)(2,1)} %bitcast.15) | data formatting | bytes 3145728
  2.5 0.0 copy-done
  2.5 0.0 copy-done.1
  2.5 0.0 copy-done.2
  2.5 0.0 copy-done.3
  2.5 0.0 copy-done.4
  2.6 0.0 copy-done.5
  2.6 13.2 %prepare.1 = (f32[16384,128]{1,0:T(8,128)S(1)}, s32[8,128]{1,0:T(8,128)S(1)}, s32[8,128]{1,0:T(8,128)S(1)}, s32[128,128]{1,0:T(8,128)S(1)}, s32[128,64]{1,0:T(8,128)S(1)}) custom-call(bf16[2048,128]{1,0:T(8,128)(2,1)S(1)} %copy-done, f32[2,4,2048]{2,1,0:T(4,128)S(1)} %copy-done.1, s32[4,2048]{1,0:T(4,128)S(1)} %bitcast.11, s32[1,128]{1,0:T(1,128)S(1)} %bitcast.14, ...), custom_call_target="tpu_custom_call" | custom-call | tf_op jit(solution)/shard_map/prepare/pallas_call | solution.py:186
  15.7 0.0 copy-done.6
  15.8 42.3 %remap.1 = (bf16[1024,128]{1,0:T(8,128)(2,1)S(1)}, f32[32,1024]{1,0:T(8,128)S(1)}) custom-call(s32[128,64]{1,0:T(8,128)S(1)} %get-tuple-element.7.src_ref, s32[8,128]{1,0:T(8,128)S(1)} %get-tuple-element.8.order_ref, s32[8,128]{1,0:T(8,128)S(1)} %get-tuple-element.9.start_ref, f32[8]{0:T(128)S(1)} %copy-done.6, f32[2048,8,128]{2,1,0:T(8,128)S(1)} %bitcast.8, ...), custom_call_target="tpu_custom_call" | custom-call | tf_op jit(solution)/shard_map/remap/pallas_call | solution.py:429
  58.0 0.7 %copy.13 = bf16[1024,128]{1,0:T(8,128)(2,1)} copy(bf16[1024,128]{1,0:T(8,128)(2,1)S(1)} %get-tuple-element.14) | data formatting | bytes 524288
  58.7 0.7 %copy.14 = f32[32,1024]{1,0:T(8,128)} copy(f32[32,1024]{1,0:T(8,128)S(1)} %get-tuple-element.15) | data formatting | bytes 262144
Async XLA Ops:
  0.6 1.9 %copy-start = (bf16[2048,128]{1,0:T(8,128)(2,1)S(1)}, bf16[2048,128]{1,0:T(8,128)(2,1)}, u32[]{:S(2)}) copy-start(bf16[2048,128]{1,0:T(8,128)(2,1)} %field_ref.1) | copy-start | bytes 1572868
  0.6 1.9 %copy-start.1 = (f32[2,4,2048]{2,1,0:T(4,128)S(1)}, f32[2,4,2048]{2,1,0:T(4,128)}, u32[]{:S(2)}) copy-start(f32[2,4,2048]{2,1,0:T(4,128)} %coef_ref.1) | copy-start | bytes 196612
  0.7 1.9 %copy-start.2 = (s32[2048,4]{0,1:T(4,128)S(1)}, s32[2048,4]{0,1:T(4,128)}, u32[]{:S(2)}) copy-start(s32[2048,4]{0,1:T(4,128)} %param.10) | copy-start | bytes 98308
  0.7 1.9 %copy-start.3 = (s32[128,64]{0,1:T(8,128)S(1)}, s32[128,64]{0,1:T(8,128)}, u32[]{:S(2)}) copy-start(s32[128,64]{0,1:T(8,128)} %param.12) | copy-start | bytes 98308
  0.7 1.9 %copy-start.4 = (s32[128,32]{0,1:T(8,128)S(1)}, s32[128,32]{0,1:T(8,128)}, u32[]{:S(2)}) copy-start(s32[128,32]{0,1:T(8,128)} %param.13) | copy-start | bytes 49156
  0.7 1.9 %copy-start.5 = (s32[128,1]{0,1:T(1,128)S(1)}, s32[128,1]{0,1:T(1,128)}, u32[]{:S(2)}) copy-start(s32[128,1]{0,1:T(1,128)} %param.14) | copy-start | bytes 1540
  0.7 15.1 %copy-start.6 = (f32[8]{0:T(128)S(1)}, f32[8]{0:T(128)}, u32[]{:S(2)}) copy-start(f32[8]{0:T(128)} %level_ref.1) | copy-start | bytes 100

commit v3 on v2

--- a/solution.py
+++ b/solution.py
@@ -45,7 +45,8 @@
     return jnp.where(mask, jnp.bfloat16(1), jnp.bfloat16(0))
 
 
-def plan(count, dest_ref, tgt_ref, src_ref, order_ref, start_ref, tags_ref, cells_ref):
+def plan(count, lines, dest_ref, tgt_ref, src_ref, order_ref, start_ref, tags_ref, cells_ref):
+    lev = lax.axis_index("lev")
     blocks = dest_ref.shape[1]
     outer, inner, plane, outers = place(count)
     steps = count // PLANE
@@ -75,11 +76,14 @@
     ahead = jnp.dot(less, ones, preferred_element_type=jnp.float32)
     starts = jnp.sum(ahead, axis=1, keepdims=True)
     rank = jnp.sum(jnp.where(hit, prefix, 0.0), axis=0, keepdims=True).astype(jnp.int32)
-    at = rank + jnp.sum(jnp.where(hit, starts, 0.0), axis=0, keepdims=True).astype(jnp.int32)
-    start_ref[...] = contract_last(
-        jnp.ones((SUB, blocks), jnp.bfloat16), ahead.astype(jnp.bfloat16)
-    ).astype(jnp.int32)
-    here = one_hot(lax.broadcasted_iota(jnp.int32, (blocks, blocks), 0) == at)
+    first = jnp.sum(jnp.where(hit, starts, 0.0), axis=0, keepdims=True).astype(jnp.int32)
+    at = rank + first
+    core = jnp.bitwise_and(at, 1)
+    turn_at = lax.shift_right_logical(at, 1) - lax.shift_right_logical(first + 1 - core, 1)
+    every = contract_last(jnp.ones((SUB, blocks), jnp.bfloat16), ahead.astype(jnp.bfloat16))
+    start_ref[...] = lax.shift_right_logical(every.astype(jnp.int32) + (1 - lev), 1)
+    half = blocks // 2
+    here = one_hot(2 * lax.broadcasted_iota(jnp.int32, (half, blocks), 0) + lev == at)
     names = lax.broadcasted_iota(jnp.int32, (SUB, blocks), 1).astype(jnp.float32)
     order_ref[...] = contract_last(names.astype(jnp.bfloat16), here).astype(jnp.int32)
     source = src_ref[...]
@@ -87,8 +91,8 @@
     moved = [contract_last(here, d.astype(jnp.float32).astype(jnp.bfloat16)) for d in digits]
     cells_ref[...] = (moved[0] * 32.0 + moved[1]).astype(jnp.int32)
 
-    line = slots * SUB + lax.shift_right_logical(rank, GROUP_BITS)
-    lane = jnp.bitwise_and(rank, GROUP - 1)
+    line = slots * SUB + core * lines + lax.shift_right_logical(turn_at, GROUP_BITS)
+    lane = jnp.bitwise_and(turn_at, GROUP - 1)
     cell = tgt_ref[...] + 1
     high = lax.shift_right_logical(cell, 5).astype(jnp.float32)
     low = jnp.bitwise_and(cell, 31).astype(jnp.float32)
@@ -105,9 +109,9 @@
 
 
 def prepare_kernel(
-    count, field_ref, coef_ref, near_ref, dest_ref, tgt_ref, src_ref,
+    count, lev_count, lines, field_ref, coef_ref, near_ref, dest_ref, tgt_ref, src_ref,
     recon, order_ref, start_ref, tags_ref, cells_ref,
-    ext, mixes, out_sem, in_sem,
+    ext, mixes, out_sem, in_sem, swap_sem,
 ):
     cells = field_ref.shape[0]
     window = TILE + 2 * HW
@@ -118,20 +122,48 @@
     left = lax.rem(me + count - 1, count)
     barrier = pltpu.get_barrier_semaphore()
     for other in (left, right):
-        pl.semaphore_signal(barrier, inc=1, device_id=(other, lev), device_id_type=MESH)
-    ext[HW:HW + cells, :] = field_ref[...]
-    plan(count, dest_ref, tgt_ref, src_ref, order_ref, start_ref, tags_ref, cells_ref)
+        for core in range(lev_count):
+            pl.semaphore_signal(barrier, inc=1, device_id=(other, core), device_id_type=MESH)
+    twin = lax.rem(lev + 1, lev_count)
+    pl.semaphore_signal(barrier, inc=1, device_id=(me, twin), device_id_type=MESH)
+    ext[lev, HW:HW + cells, :] = field_ref[...]
+    pl.semaphore_wait(barrier, 2 * lev_count + 1)
+    swap = pltpu.make_async_remote_copy(
+        src_ref=field_ref, dst_ref=ext.at[lev, pl.ds(HW, cells)],
+        send_sem=swap_sem.at[0], recv_sem=swap_sem.at[1],
+        device_id=(me, twin), device_id_type=MESH,
+    )
+    swap.start()
+
+    def edge(side, core, source):
+        return pltpu.make_async_remote_copy(
+            src_ref=field_ref.at[pl.ds((1 - side) * (cells - HW), HW)],
+            dst_ref=ext.at[source, pl.ds(side * (HW + cells), HW)],
+            send_sem=out_sem.at[side, core], recv_sem=in_sem.at[side, source],
+            device_id=((right, left)[side], core), device_id_type=MESH,
+        )
+
+    for side in range(2):
+        for core in range(lev_count):
+            edge(side, core, lev).start()
+    plan(count, lines, dest_ref, tgt_ref, src_ref, order_ref, start_ref, tags_ref, cells_ref)
+
+    columns = field_ref.shape[1]
+
+    def put(at, parts):
+        for h in range(lev_count):
+            recon[h, pl.ds(at, TILE, stride=SUB), :] = parts[h].astype(jnp.float32)
 
     def tile(t):
         base = pl.multiple_of(t * TILE, TILE)
         near = near_ref[:, pl.ds(base, TILE)] - base
         coef = [coef_ref[g, :, pl.ds(base, TILE)] for g in range(2)]
         totals = [-jnp.sum(coef[g], axis=0, keepdims=True) for g in range(2)]
-        held = ext[pl.ds(base, window), :]
+        held = jnp.concatenate(
+            [ext[h, pl.ds(base, window), :] for h in range(lev_count)], axis=1
+        )
         rows = pl.multiple_of(base * SUB, TILE * SUB)
-        recon[pl.ds(rows, TILE, stride=SUB), :] = field_ref[pl.ds(base, TILE), :].astype(
-            jnp.float32
-        )
+        put(rows, [ext[h, pl.ds(base + HW, TILE), :] for h in range(lev_count)])
         for w in range(0, window, PIECE):
             here = lax.broadcasted_iota(jnp.int32, (PIECE, TILE), 0) + w
             own = here == lax.broadcasted_iota(jnp.int32, (PIECE, TILE), 1) + HW
@@ -148,60 +180,47 @@
         for g in range(2):
             value = contract_first(mixes[:, 2 * g * TILE:(2 * g + 1) * TILE], held)
             value = value + contract_first(mixes[:, (2 * g + 1) * TILE:(2 * g + 2) * TILE], held)
-            recon[pl.ds(rows + 1 + g, TILE, stride=SUB), :] = value
-
-    @pl.loop(1, tiles // 2)
+            put(rows + 1 + g, [value[:, h * columns:(h + 1) * columns] for h in range(lev_count)])
+
+    swap.wait()
+
+    @pl.loop(1, tiles - 1)
     def _(t):
         tile(t)
 
-    pl.semaphore_wait(barrier, 2)
-    low = pltpu.make_async_remote_copy(
-        src_ref=field_ref.at[pl.ds(cells - HW, HW)], dst_ref=ext.at[pl.ds(0, HW)],
-        send_sem=out_sem.at[0], recv_sem=in_sem.at[0],
-        device_id=(right, lev), device_id_type=MESH,
-    )
-    high = pltpu.make_async_remote_copy(
-        src_ref=field_ref.at[pl.ds(0, HW)], dst_ref=ext.at[pl.ds(HW + cells, HW)],
-        send_sem=out_sem.at[1], recv_sem=in_sem.at[1],
-        device_id=(left, lev), device_id_type=MESH,
-    )
-    low.start()
-    high.start()
-
-    @pl.loop(tiles // 2, tiles - 1)
-    def _(t):
-        tile(t)
-
-    low.wait()
-    high.wait()
+    for side in range(2):
+        for core in range(lev_count):
+            edge(side, core, core).wait()
 
     @pl.loop(0, 2)
     def _(e):
         tile(e * (tiles - 1))
 
 
-def prepare(count, field, coef, near_t, dest_t, tgt_t, src_t):
+def prepare(count, lev_count, lines, field, coef, near_t, dest_t, tgt_t, src_t):
     cells, columns = field.shape
+    half = dest_t.shape[1] // 2
     vmem = pl.BlockSpec(memory_space=pltpu.VMEM)
     return pl.pallas_call(
-        functools.partial(prepare_kernel, count),
+        functools.partial(prepare_kernel, count, lev_count, lines),
         out_shape=(
-            jax.ShapeDtypeStruct((cells * SUB, columns), jnp.float32),
-            jax.ShapeDtypeStruct((SUB, dest_t.shape[1]), jnp.int32),
+            jax.ShapeDtypeStruct((lev_count, cells * SUB, columns), jnp.float32),
+            jax.ShapeDtypeStruct((SUB, half), jnp.int32),
             jax.ShapeDtypeStruct((SUB, max(count, LANES)), jnp.int32),
             jax.ShapeDtypeStruct((count * SUB, LANES), jnp.int32),
-            jax.ShapeDtypeStruct(src_t.shape[::-1], jnp.int32),
+            jax.ShapeDtypeStruct((half, src_t.shape[0]), jnp.int32),
         ),
         in_specs=[vmem] * 6,
         out_specs=(vmem,) * 5,
         scratch_shapes=[
-            pltpu.VMEM((cells + 2 * HW, columns), jnp.bfloat16),
+            pltpu.VMEM((lev_count, cells + 2 * HW, columns), jnp.bfloat16),
             pltpu.VMEM((TILE + 2 * HW, 4 * TILE), jnp.bfloat16),
-            pltpu.SemaphoreType.DMA((2,)),
+            pltpu.SemaphoreType.DMA((2, lev_count)),
+            pltpu.SemaphoreType.DMA((2, lev_count)),
             pltpu.SemaphoreType.DMA((2,)),
         ],
         compiler_params=pltpu.CompilerParams(
-            vmem_limit_bytes=24 << 20, collective_id=1, has_side_effects=True
+            vmem_limit_bytes=28 << 20, collective_id=1, has_side_effects=True
         ),
         name="prepare",
     )(field, coef, near_t, dest_t, tgt_t, src_t)
@@ -223,7 +242,7 @@
     width = min(LANES, rows)
     lines = rows // width
     targets, columns = total.shape
-    partner_lev = lax.rem(lev + 1, lev_count)
+    twin = lax.rem(lev + 1, lev_count)
     peers = [
         base + PLANE - 1 - plane,
         base + plane + 1 - 2 * lax.rem(plane, 2),
@@ -235,21 +254,23 @@
         return lax.rem(outer + turn, outers) * PLANE * PAIR + inner * PLANE + plane
 
     barrier = pltpu.get_barrier_semaphore()
-    for other in peers + [partner]:
-        pl.semaphore_signal(barrier, inc=1, device_id=(other, lev), device_id_type=MESH)
+    for other in peers:
+        for core in range(lev_count):
+            pl.semaphore_signal(barrier, inc=1, device_id=(other, core), device_id_type=MESH)
+    pl.semaphore_signal(barrier, inc=1, device_id=(partner, lev), device_id_type=MESH)
 
     @pl.loop(1, outers)
     def _(t):
         pl.semaphore_signal(barrier, inc=1, device_id=(mirror(t), lev), device_id_type=MESH)
 
-    pl.semaphore_signal(barrier, inc=1, device_id=(me, partner_lev), device_id_type=MESH)
-
-    @pl.loop(0, compact.shape[0] // SUB)
+    pl.semaphore_signal(barrier, inc=1, device_id=(me, twin), device_id_type=MESH)
+
+    @pl.loop(0, compact.shape[1] // SUB)
     def _(n):
-        compact[pl.ds(n * SUB, SUB)] = jnp.zeros((SUB, TB, columns), jnp.bfloat16)
+        compact[:, pl.ds(n * SUB, SUB)] = jnp.zeros((lev_count, SUB, TB, columns), jnp.bfloat16)
 
     seen[PLANE - 1] = tags_ref[PLANE - 1]
-    pl.semaphore_wait(barrier, PLANE + outers)
+    pl.semaphore_wait(barrier, (PLANE - 1) * lev_count + 1 + outers)
 
     def tag_copy(spot):
         return pltpu.make_async_remote_copy(
@@ -258,11 +279,11 @@
             device_id=(peers[spot], lev), device_id_type=MESH,
         )
 
-    def chunk_copy(step, spot):
+    def chunk_copy(step, spot, core, source):
         return pltpu.make_async_remote_copy(
-            src_ref=staged.at[step, spot], dst_ref=land.at[step, spot],
-            send_sem=chunk_out.at[step, spot], recv_sem=chunk_in.at[step, spot],
-            device_id=(peers[spot], lev), device_id_type=MESH,
+            src_ref=staged.at[step, spot, core], dst_ref=land.at[step, spot, source],
+            send_sem=chunk_out.at[step, spot, core], recv_sem=chunk_in.at[step, spot, source],
+            device_id=((peers + [me])[spot], core), device_id_type=MESH,
         )
 
     def line_copy(step, to):
@@ -280,30 +301,43 @@
             for m in range(unroll):
                 index = src_ref.at[first + m]
                 buffer = picked.at[m]
-                found = [recon[index[begin + j]] for j in range(BATCH)]
+                found = [
+                    [recon[h, index[begin + j]] for h in range(lev_count)] for j in range(BATCH)
+                ]
                 for j in range(BATCH):
                     to = ((begin + j) % GROUP) * (SB // GROUP) + (begin + j) // GROUP
-                    buffer[pl.ds(to, 3, stride=SPAN), :] = found[j][0:3, :]
+                    for h in range(lev_count):
+                        buffer[h, pl.ds(to, 3, stride=SPAN), :] = found[j][h][0:3, :]
 
     def one(i, buffer):
         held = weight_ref[order_ref[0, i]]
         whole = None
         for q in range(GROUP):
-            parts = [
-                buffer[pl.ds(c * SPAN + q * (SB // GROUP), SB // GROUP), :] for c in range(3)
-            ]
-            terms = jnp.concatenate(parts, axis=0).astype(jnp.bfloat16)
+            sides = []
+            for h in range(lev_count):
+                parts = [
+                    buffer[h, pl.ds(c * SPAN + q * (SB // GROUP), SB // GROUP), :]
+                    for c in range(3)
+                ]
+                sides.append(jnp.concatenate(parts, axis=0).astype(jnp.bfloat16))
+            terms = jnp.concatenate(sides, axis=1)
             product = contract_first(held[:, q * TB:(q + 1) * TB], terms)
             whole = product if whole is None else whole + product
-        compact[i] = whole.astype(jnp.bfloat16)
+        for h in range(lev_count):
+            compact[h, i] = whole[:, h * columns:(h + 1) * columns].astype(jnp.bfloat16)
 
     def stage(step, spot):
-        chunk = compact[pl.ds(start_ref[0, step * PLANE + spot], capacity)].reshape(rows, columns)
+        first = start_ref[0, step * PLANE + spot]
         if spot < PLANE - 1:
-            staged[step, spot] = chunk
-            chunk_copy(step, spot).start()
+            for core in range(lev_count):
+                staged[step, spot, core] = compact[core, pl.ds(first, capacity)].reshape(
+                    rows, columns
+                )
+                chunk_copy(step, spot, core, lev).start()
         else:
-            land[step, spot] = chunk
+            land[step, spot, lev] = compact[lev, pl.ds(first, capacity)].reshape(rows, columns)
+            staged[step, spot, twin] = compact[twin, pl.ds(first, capacity)].reshape(rows, columns)
+            chunk_copy(step, spot, twin, lev).start()
 
     unroll = min(UNROLL, capacity)
 
@@ -332,27 +366,24 @@
         cell = seen[spot, step]
         part = lax.shift_right_arithmetic(cell, 8)
         low = jnp.bitwise_and(cell, BAND - 1)
-        chunk = land[step, spot]
+        chunk = land[step, spot].reshape(lev_count * rows, columns)
         where = lax.broadcasted_iota(jnp.int32, (BAND, width), 0).astype(jnp.float32)
         where = where.astype(jnp.bfloat16)
         for h in range(targets // BAND):
             mark = jnp.where(part == h, low, -1).astype(jnp.float32).astype(jnp.bfloat16)
-            hits = [
-                one_hot(where == mark[m:m + 1, :width]) for m in range(lines)
-            ]
-            hits = hits[0] if lines == 1 else jnp.concatenate(hits, axis=1)
+            hits = jnp.concatenate(
+                [one_hot(where == mark[m:m + 1, :width]) for m in range(lev_count * lines)], axis=1
+            )
             sums = jnp.dot(hits, chunk, preferred_element_type=jnp.float32)
             band = pl.ds(h * BAND, BAND)
             total[band, :] = sums if fresh else total[band, :] + sums
 
     def gather(step):
+        chunk_copy(step, PLANE - 1, twin, twin).wait_recv()
         add(step, PLANE - 1, True)
         for spot in range(PLANE - 1):
-
-            def ready(spot=spot):
-                chunk_copy(step, spot).wait_recv()
-
-            ready()
+            for core in range(lev_count):
+                chunk_copy(step, spot, core, core).wait_recv()
             add(step, spot, False)
 
     def near(step):
@@ -397,7 +428,7 @@
     )
     swap = pltpu.make_async_remote_copy(
         src_ref=local_sum, dst_ref=other_sum, send_sem=sum_sem.at[0], recv_sem=sum_sem.at[1],
-        device_id=(me, partner_lev), device_id_type=MESH,
+        device_id=(me, twin), device_id_type=MESH,
     )
     swap.start()
     for spot in range(PLANE - 1):
@@ -406,7 +437,9 @@
     @pl.loop(0, steps)
     def _(step):
         for spot in range(PLANE - 1):
-            chunk_copy(step, spot).wait_send()
+            for core in range(lev_count):
+                chunk_copy(step, spot, core, lev).wait_send()
+        chunk_copy(step, PLANE - 1, twin, lev).wait_send()
 
     @pl.loop(0, steps - 1)
     def _(step):
@@ -417,14 +450,14 @@
 
 
 def remap(count, capacity, lev_count, level_count, cells, order, start, level, recon, weight, tags):
-    columns = recon.shape[2]
+    columns = recon.shape[3]
     blocks = cells.shape[0]
     steps = count // PLANE
     rows = capacity * TB
     smem = pl.BlockSpec(memory_space=pltpu.SMEM)
     vmem = pl.BlockSpec(memory_space=pltpu.VMEM)
     dma = pltpu.SemaphoreType.DMA
-    chunk = (rows, columns)
+    chunk = (lev_count, rows, columns)
     dense = (T_DEV, columns)
     return pl.pallas_call(
         functools.partial(remap_kernel, count, capacity, level_count, lev_count),
@@ -435,9 +468,9 @@
         in_specs=[smem] * 4 + [vmem] * 3,
         out_specs=(vmem, vmem),
         scratch_shapes=[
-            pltpu.VMEM((UNROLL, 3 * SPAN, columns), jnp.float32),
-            pltpu.VMEM((-(-(blocks + capacity) // SUB) * SUB, TB, columns), jnp.bfloat16),
-            pltpu.VMEM((steps, PLANE - 1) + chunk, jnp.bfloat16),
+            pltpu.VMEM((UNROLL, lev_count, 3 * SPAN, columns), jnp.float32),
+            pltpu.VMEM((lev_count, -(-(blocks + capacity) // SUB) * SUB, TB, columns), jnp.bfloat16),
+            pltpu.VMEM((steps, PLANE) + chunk, jnp.bfloat16),
             pltpu.VMEM((steps, PLANE) + chunk, jnp.bfloat16),
             pltpu.VMEM((PLANE, steps, SUB, LANES), jnp.int32),
             pltpu.VMEM(dense, jnp.float32),
@@ -445,8 +478,8 @@
             pltpu.VMEM((steps - 1,) + dense, jnp.bfloat16),
             pltpu.VMEM((FIELDS, T_DEV), jnp.float32),
             pltpu.VMEM((FIELDS, T_DEV), jnp.float32),
-            dma((steps, PLANE - 1)),
-            dma((steps, PLANE - 1)),
+            dma((steps, PLANE, lev_count)),
+            dma((steps, PLANE, lev_count)),
             dma((PLANE - 1,)),
             dma((PLANE - 1,)),
             dma((steps - 1,)),
@@ -454,7 +487,7 @@
             dma((2,)),
         ],
         compiler_params=pltpu.CompilerParams(
-            vmem_limit_bytes=(12 << 20) + steps * (3 << 18), collective_id=0, has_side_effects=True
+            vmem_limit_bytes=(16 << 20) + steps * (3 << 18), collective_id=0, has_side_effects=True
         ),
         name="remap",
     )(cells, order, start, level, recon, weight, tags)
@@ -464,15 +497,18 @@
     count = lax.axis_size("src")
     columns = field.shape[1]
     blocks = src_index.shape[0]
-    capacity = 2 * blocks // count
+    lev_count = lax.axis_size("lev")
+    capacity = 2 * blocks // count // lev_count
+    lines = -(-capacity // GROUP)
     steps = count // PLANE
     shaped = weights.reshape(blocks, 3 * SB * TB // LANES, LANES)
     recon, order, start, tags, cells = prepare(
-        count, field, grad_coef, neighbours.T, block_dest.T, tgt_index.T, src_index.T
+        count, lev_count, lines, field, grad_coef, neighbours.T, block_dest.T, tgt_index.T,
+        src_index.T,
     )
     return remap(
-        count, capacity, lax.axis_size("lev"), columns // FIELDS, cells, order, start,
-        level_weight, recon.reshape(-1, SUB, columns), shaped, tags.reshape(PLANE, steps, SUB, LANES),
+        count, capacity, lev_count, columns // FIELDS, cells, order, start,
+        level_weight, recon.reshape(lev_count, -1, SUB, columns), shaped, tags.reshape(PLANE, steps, SUB, LANES),
     )
 
 

time: 59.5 us -> 56.6 us (0.951); the launches traced: 59.4 us -> 55.6 us
  Pallas kernels: 55.4 us -> 51.6 us
    pallas_call x1, Pallas kernels: 42.3 us -> 35.5 us  [remap(): pl.pallas_call(functools.partial(remap_kernel, count, capacity, level_cou...]
    pallas_call x1, Pallas kernels: 13.2 us -> 16.1 us  [prepare(): pl.pallas_call(functools.partial(prepare_kernel, count, lev_count, lines)...]
where the time goes in v3:
time: 56.6 us; the launch traced here: 55.6 us
  Pallas kernels  51.6 us (91%)
  local copies, waits for them, and re-layouts  3.19 us (6%)
  between operations  0.77 us (1%)
    pallas_call x1, Pallas kernels, remap(): pl.pallas_call(functools.partial(remap_kernel, count, capacity, level_cou...  35.5 us
    pallas_call x1, Pallas kernels, prepare(): pl.pallas_call(functools.partial(prepare_kernel, count, lev_count, lines)...  16.1 us
    unnamed x17, local copies, waits for them, and re-layouts  3.19 us

profile of v3, /device:TPU:0, one launch (start us, length us, event | category | flops | bytes accessed | tf_op | source)
XLA Modules:
  0.0 55.6 jit_solution(18091566065113508044)
XLA Ops:
  0.6 0.0 copy-start
  0.6 0.0 copy-start.1
  0.7 0.0 copy-start.2
  0.7 0.0 copy-start.3
  0.7 0.0 copy-start.4
  0.7 0.0 copy-start.6
  0.7 0.0 copy-start.5
  0.7 1.8 %copy.10 = bf16[16,8,48,128]{3,2,1,0:T(8,128)(2,1)S(1)} copy(bf16[16,8,48,128]{3,1,2,0:T(8,128)(2,1)} %bitcast.15) | data formatting | bytes 3145728
  2.5 0.0 copy-done
  2.5 0.0 copy-done.1
  2.5 0.0 copy-done.2
  2.5 0.0 copy-done.3
  2.5 0.0 copy-done.4
  2.6 0.0 copy-done.6
  2.6 16.1 %prepare.1 = (f32[2,16384,128]{2,1,0:T(8,128)S(1)}, s32[8,64]{1,0:T(8,128)S(1)}, s32[8,128]{1,0:T(8,128)S(1)}, s32[128,128]{1,0:T(8,128)S(1)}, s32[64,64]{1,0:T(8,128)S(1)}) custom-call(bf16[2048,128]{1,0:T(8,128)(2,1)S(1)} %copy-done, f32[2,4,2048]{2,1,0:T(4,128)S(1)} %copy-done.1, s32[4,2048]{1,0:T(4,128)S(1)} %bitcast.11, s32[1,128]{1,0:T(1,128)S(1)} %bitcast.14, ...), custom_call_target="tpu_custom_call" | custom-call | tf_op jit(solution)/shard_map/prepare/pallas_call | solution.py:204
  18.7 0.0 copy-done.5
  18.7 35.5 %remap.1 = (bf16[1024,128]{1,0:T(8,128)(2,1)S(1)}, f32[32,1024]{1,0:T(8,128)S(1)}) custom-call(s32[64,64]{1,0:T(8,128)S(1)} %get-tuple-element.7.src_ref, s32[8,64]{1,0:T(8,128)S(1)} %get-tuple-element.8.order_ref, s32[8,128]{1,0:T(8,128)S(1)} %get-tuple-element.9.start_ref, f32[8]{0:T(128)S(1)} %copy-done.5, f32[2,2048,8,128]{3,2,1,0:T(8,128)S(1)} %bitcast.8, ...), custom_call_target="tpu_custom_call" | custom-call | tf_op jit(solution)/shard_map/remap/pallas_call | solution.py:462
  54.2 0.7 %copy.13 = bf16[1024,128]{1,0:T(8,128)(2,1)} copy(bf16[1024,128]{1,0:T(8,128)(2,1)S(1)} %get-tuple-element.14) | data formatting | bytes 524288
  54.9 0.7 %copy.14 = f32[32,1024]{1,0:T(8,128)} copy(f32[32,1024]{1,0:T(8,128)S(1)} %get-tuple-element.15) | data formatting | bytes 262144
Async XLA Ops:
  0.6 1.9 %copy-start = (bf16[2048,128]{1,0:T(8,128)(2,1)S(1)}, bf16[2048,128]{1,0:T(8,128)(2,1)}, u32[]{:S(2)}) copy-start(bf16[2048,128]{1,0:T(8,128)(2,1)} %field_ref.1) | copy-start | bytes 1572868
  0.6 1.9 %copy-start.1 = (f32[2,4,2048]{2,1,0:T(4,128)S(1)}, f32[2,4,2048]{2,1,0:T(4,128)}, u32[]{:S(2)}) copy-start(f32[2,4,2048]{2,1,0:T(4,128)} %coef_ref.1) | copy-start | bytes 196612
  0.7 1.9 %copy-start.2 = (s32[2048,4]{0,1:T(4,128)S(1)}, s32[2048,4]{0,1:T(4,128)}, u32[]{:S(2)}) copy-start(s32[2048,4]{0,1:T(4,128)} %param.10) | copy-start | bytes 98308
  0.7 1.9 %copy-start.3 = (s32[128,64]{0,1:T(8,128)S(1)}, s32[128,64]{0,1:T(8,128)}, u32[]{:S(2)}) copy-start(s32[128,64]{0,1:T(8,128)} %param.12) | copy-start | bytes 98308
  0.7 1.9 %copy-start.4 = (s32[128,32]{0,1:T(8,128)S(1)}, s32[128,32]{0,1:T(8,128)}, u32[]{:S(2)}) copy-start(s32[128,32]{0,1:T(8,128)} %param.13) | copy-start | bytes 49156
  0.7 1.9 %copy-start.6 = (s32[128,1]{0,1:T(1,128)S(1)}, s32[128,1]{0,1:T(1,128)}, u32[]{:S(2)}) copy-start(s32[128,1]{0,1:T(1,128)} %param.14) | copy-start | bytes 1540
  0.7 18.0 %copy-start.5 = (f32[8]{0:T(128)S(1)}, f32[8]{0:T(128)}, u32[]{:S(2)}) copy-start(f32[8]{0:T(128)} %level_ref.1) | copy-start | bytes 100

commit v4 on v3

--- a/solution.py
+++ b/solution.py
@@ -231,7 +231,7 @@
     src_ref, order_ref, start_ref, level_ref, recon, weight_ref, tags_ref,
     remapped_ref, sum_ref,
     picked, compact, staged, land, seen, total, dense_out, dense_in, local_sum, other_sum,
-    chunk_out, chunk_in, tag_out, tag_in, line_out, line_in, sum_sem,
+    chunk_out, chunk_in, tag_out, tag_in, line_out, line_in, sum_out, sum_in,
 ):
     me = lax.axis_index("src")
     lev = lax.axis_index("lev")
@@ -241,7 +241,7 @@
     rows = capacity * TB
     width = min(LANES, rows)
     lines = rows // width
-    targets, columns = total.shape
+    bands, _, columns = remapped_ref.shape
     twin = lax.rem(lev + 1, lev_count)
     peers = [
         base + PLANE - 1 - plane,
@@ -286,11 +286,18 @@
             device_id=((peers + [me])[spot], core), device_id_type=MESH,
         )
 
-    def line_copy(step, to):
+    def line_copy(step, band, to):
         return pltpu.make_async_remote_copy(
-            src_ref=dense_out.at[step], dst_ref=dense_in.at[step],
-            send_sem=line_out.at[step], recv_sem=line_in.at[step],
+            src_ref=dense_out.at[step, band], dst_ref=dense_in.at[step, band],
+            send_sem=line_out.at[step, band], recv_sem=line_in.at[step, band],
             device_id=(to, lev), device_id_type=MESH,
+        )
+
+    def swap(band):
+        return pltpu.make_async_remote_copy(
+            src_ref=local_sum.at[band], dst_ref=other_sum.at[band],
+            send_sem=sum_out.at[band], recv_sem=sum_in.at[band],
+            device_id=(me, twin), device_id_type=MESH,
         )
 
     for spot in range(PLANE - 1):
@@ -354,83 +361,98 @@
 
             stage(step, spot)
 
-    @pl.loop(steps // 2, steps)
-    def _(step):
+    def stage_all(step):
         for spot in range(PLANE):
             stage(step, spot)
 
+    @pl.loop(steps // 2, steps - 1)
+    def _(step):
+        stage_all(step)
+
     for spot in range(PLANE - 1):
         tag_copy(spot).wait_recv()
 
-    def add(step, spot, fresh):
-        cell = seen[spot, step]
-        part = lax.shift_right_arithmetic(cell, 8)
-        low = jnp.bitwise_and(cell, BAND - 1)
-        chunk = land[step, spot].reshape(lev_count * rows, columns)
+    def ready(step):
+        for spot in range(PLANE - 1):
+            for core in range(lev_count):
+                chunk_copy(step, spot, core, core).wait_recv()
+        chunk_copy(step, PLANE - 1, twin, twin).wait_recv()
+
+    def gather(step, band):
         where = lax.broadcasted_iota(jnp.int32, (BAND, width), 0).astype(jnp.float32)
         where = where.astype(jnp.bfloat16)
-        for h in range(targets // BAND):
-            mark = jnp.where(part == h, low, -1).astype(jnp.float32).astype(jnp.bfloat16)
+        sums = None
+        for spot in range(PLANE):
+            cell = seen[spot, step]
+            part = lax.shift_right_arithmetic(cell, 8)
+            low = jnp.bitwise_and(cell, BAND - 1)
+            chunk = land[step, spot].reshape(lev_count * rows, columns)
+            mark = jnp.where(part == band, low, -1).astype(jnp.float32).astype(jnp.bfloat16)
             hits = jnp.concatenate(
                 [one_hot(where == mark[m:m + 1, :width]) for m in range(lev_count * lines)], axis=1
             )
-            sums = jnp.dot(hits, chunk, preferred_element_type=jnp.float32)
-            band = pl.ds(h * BAND, BAND)
-            total[band, :] = sums if fresh else total[band, :] + sums
-
-    def gather(step):
-        chunk_copy(step, PLANE - 1, twin, twin).wait_recv()
-        add(step, PLANE - 1, True)
-        for spot in range(PLANE - 1):
-            for core in range(lev_count):
-                chunk_copy(step, spot, core, core).wait_recv()
-            add(step, spot, False)
+            term = jnp.dot(hits, chunk, preferred_element_type=jnp.float32)
+            sums = term if sums is None else sums + term
+        return sums
 
     def near(step):
-        gather(step)
-        dense_out[step] = total[...].astype(jnp.bfloat16)
-        line_copy(step, partner).start()
+        ready(step)
+
+        @pl.loop(0, bands)
+        def _(band):
+            dense_out[step, band] = gather(step, band).astype(jnp.bfloat16)
+            line_copy(step, band, partner).start()
 
     @pl.loop(0, outers - 1)
     def _(turn):
         step = 2 * turn
         near(step)
-        gather(step + 1)
-        line_copy(step, partner).wait_recv()
-        both = total[...] + dense_in[step].astype(jnp.float32)
-        dense_out[step + 1] = both.astype(jnp.bfloat16)
-        line_copy(step + 1, mirror(turn + 1)).start()
+        ready(step + 1)
+
+        @pl.loop(0, bands)
+        def _(band):
+            @pl.when(jnp.logical_and(turn == 0, band == bands // 2))
+            def _():
+                stage_all(steps - 1)
+
+            sums = gather(step + 1, band)
+            line_copy(step, band, partner).wait_recv()
+            dense_out[step + 1, band] = (
+                sums + dense_in[step, band].astype(jnp.float32)
+            ).astype(jnp.bfloat16)
+            line_copy(step + 1, band, mirror(turn + 1)).start()
 
     near(steps - 2)
-    gather(steps - 1)
-    line_copy(steps - 2, partner).wait_recv()
-    total[...] += dense_in[steps - 2].astype(jnp.float32)
-
-    @pl.loop(0, outers - 1)
-    def _(turn):
-        line_copy(2 * turn + 1, mirror(turn + 1)).wait_recv()
-        total[...] += dense_in[2 * turn + 1].astype(jnp.float32)
-
-    result = total[...]
-    remapped_ref[...] = result.astype(jnp.bfloat16)
+    ready(steps - 1)
     start = lev * level_count
     which = lax.broadcasted_iota(jnp.int32, (FIELDS, columns), 1)
     line = lax.broadcasted_iota(jnp.int32, (FIELDS, columns), 0)
     mix = jnp.zeros((FIELDS, columns), jnp.float32)
     for l in range(level_count):
         mix = jnp.where(which == line + l * FIELDS, level_ref[start + l], mix)
-    local_sum[...] = lax.dot_general(
-        mix,
-        result,
-        (((1,), (1,)), ((), ())),
-        precision=lax.Precision.HIGHEST,
-        preferred_element_type=jnp.float32,
-    )
-    swap = pltpu.make_async_remote_copy(
-        src_ref=local_sum, dst_ref=other_sum, send_sem=sum_sem.at[0], recv_sem=sum_sem.at[1],
-        device_id=(me, twin), device_id_type=MESH,
-    )
-    swap.start()
+
+    @pl.loop(0, bands)
+    def _(band):
+        total[...] = gather(steps - 1, band)
+        line_copy(steps - 2, band, partner).wait_recv()
+        total[...] += dense_in[steps - 2, band].astype(jnp.float32)
+
+        @pl.loop(0, outers - 1)
+        def _(turn):
+            line_copy(2 * turn + 1, band, mirror(turn + 1)).wait_recv()
+            total[...] += dense_in[2 * turn + 1, band].astype(jnp.float32)
+
+        result = total[...]
+        remapped_ref[band] = result.astype(jnp.bfloat16)
+        local_sum[band] = lax.dot_general(
+            mix,
+            result,
+            (((1,), (1,)), ((), ())),
+            precision=lax.Precision.HIGHEST,
+            preferred_element_type=jnp.float32,
+        )
+        swap(band).start()
+
     for spot in range(PLANE - 1):
         tag_copy(spot).wait_send()
 
@@ -443,10 +465,12 @@
 
     @pl.loop(0, steps - 1)
     def _(step):
-        line_copy(step, partner).wait_send()
-
-    swap.wait()
-    sum_ref[...] = local_sum[...] + other_sum[...]
+        for band in range(bands):
+            line_copy(step, band, partner).wait_send()
+
+    for band in range(bands):
+        swap(band).wait()
+        sum_ref[:, band * BAND:(band + 1) * BAND] = local_sum[band] + other_sum[band]
 
 
 def remap(count, capacity, lev_count, level_count, cells, order, start, level, recon, weight, tags):
@@ -458,7 +482,8 @@
     vmem = pl.BlockSpec(memory_space=pltpu.VMEM)
     dma = pltpu.SemaphoreType.DMA
     chunk = (lev_count, rows, columns)
-    dense = (T_DEV, columns)
+    bands = T_DEV // BAND
+    dense = (bands, BAND, columns)
     return pl.pallas_call(
         functools.partial(remap_kernel, count, capacity, level_count, lev_count),
         out_shape=(
@@ -473,18 +498,19 @@
             pltpu.VMEM((steps, PLANE) + chunk, jnp.bfloat16),
             pltpu.VMEM((steps, PLANE) + chunk, jnp.bfloat16),
             pltpu.VMEM((PLANE, steps, SUB, LANES), jnp.int32),
-            pltpu.VMEM(dense, jnp.float32),
+            pltpu.VMEM((BAND, columns), jnp.float32),
             pltpu.VMEM((steps - 1,) + dense, jnp.bfloat16),
             pltpu.VMEM((steps - 1,) + dense, jnp.bfloat16),
-            pltpu.VMEM((FIELDS, T_DEV), jnp.float32),
-            pltpu.VMEM((FIELDS, T_DEV), jnp.float32),
+            pltpu.VMEM((bands, FIELDS, BAND), jnp.float32),
+            pltpu.VMEM((bands, FIELDS, BAND), jnp.float32),
             dma((steps, PLANE, lev_count)),
             dma((steps, PLANE, lev_count)),
             dma((PLANE - 1,)),
             dma((PLANE - 1,)),
-            dma((steps - 1,)),
-            dma((steps - 1,)),
-            dma((2,)),
+            dma((steps - 1, bands)),
+            dma((steps - 1, bands)),
+            dma((bands,)),
+            dma((bands,)),
         ],
         compiler_params=pltpu.CompilerParams(
             vmem_limit_bytes=(16 << 20) + steps * (3 << 18), collective_id=0, has_side_effects=True
@@ -506,10 +532,11 @@
         count, lev_count, lines, field, grad_coef, neighbours.T, block_dest.T, tgt_index.T,
         src_index.T,
     )
-    return remap(
+    remapped, sums = remap(
         count, capacity, lev_count, columns // FIELDS, cells, order, start,
         level_weight, recon.reshape(lev_count, -1, SUB, columns), shaped, tags.reshape(PLANE, steps, SUB, LANES),
     )
+    return remapped.reshape(T_DEV, columns), sums
 
 
 def solution(mesh):

time: 56.6 us -> 56.3 us (level)
  the two profiles are of different devices: /device:TPU:0 before, /device:TPU:3 now
where the time goes in v4:
time: 56.3 us; the launch traced here: 56.2 us
  Pallas kernels  52.2 us (93%)
  local copies, waits for them, and re-layouts  3.19 us (6%)
  between operations  0.77 us (1%)
    pallas_call x1, Pallas kernels, remap(): pl.pallas_call(functools.partial(remap_kernel, count, capacity, level_cou...  41 us
    pallas_call x1, Pallas kernels, prepare(): pl.pallas_call(functools.partial(prepare_kernel, count, lev_count, lines)...  11.2 us
    unnamed x17, local copies, waits for them, and re-layouts  3.19 us

profile of v4, /device:TPU:3, one launch (start us, length us, event | category | flops | bytes accessed | tf_op | source)
XLA Modules:
  0.0 56.2 jit_solution(18229070065164757389)
XLA Ops:
  0.6 0.0 copy-start
  0.6 0.0 copy-start.1
  0.7 0.0 copy-start.2
  0.7 0.0 copy-start.3
  0.7 0.0 copy-start.4
  0.7 0.0 copy-start.6
  0.7 0.0 copy-start.5
  0.7 1.8 %copy.10 = bf16[16,8,48,128]{3,2,1,0:T(8,128)(2,1)S(1)} copy(bf16[16,8,48,128]{3,1,2,0:T(8,128)(2,1)} %bitcast.17) | data formatting | bytes 3145728
  2.5 0.0 copy-done
  2.5 0.0 copy-done.1
  2.5 0.0 copy-done.2
  2.5 0.0 copy-done.3
  2.5 0.0 copy-done.4
  2.6 0.0 copy-done.6
  2.6 11.2 %prepare.1 = (f32[2,16384,128]{2,1,0:T(8,128)S(1)}, s32[8,64]{1,0:T(8,128)S(1)}, s32[8,128]{1,0:T(8,128)S(1)}, s32[128,128]{1,0:T(8,128)S(1)}, s32[64,64]{1,0:T(8,128)S(1)}) custom-call(bf16[2048,128]{1,0:T(8,128)(2,1)S(1)} %copy-done, f32[2,4,2048]{2,1,0:T(4,128)S(1)} %copy-done.1, s32[4,2048]{1,0:T(4,128)S(1)} %bitcast.13, s32[1,128]{1,0:T(1,128)S(1)} %bitcast.16, ...), custom_call_target="tpu_custom_call" | custom-call | tf_op jit(solution)/shard_map/prepare/pallas_call | solution.py:204
  13.8 0.0 copy-done.5
  13.8 41.0 %remap.1 = (bf16[4,256,128]{2,1,0:T(8,128)(2,1)S(1)}, f32[32,1024]{1,0:T(8,128)S(1)}) custom-call(s32[64,64]{1,0:T(8,128)S(1)} %get-tuple-element.9.src_ref, s32[8,64]{1,0:T(8,128)S(1)} %get-tuple-element.10.order_ref, s32[8,128]{1,0:T(8,128)S(1)} %get-tuple-element.11.start_ref, f32[8]{0:T(128)S(1)} %copy-done.5, f32[2,2048,8,128]{3,2,1,0:T(8,128)S(1)} %bitcast.9, ...), custom_call_target="tpu_custom_call" | custom-call | tf_op jit(solution)/shard_map/remap/pallas_call | solution.py:487
  54.8 0.7 %copy.13 = bf16[1024,128]{1,0:T(8,128)(2,1)} copy(bf16[1024,128]{1,0:T(8,128)(2,1)S(1)} %bitcast.11) | data formatting | bytes 524288
  55.5 0.7 %copy.14 = f32[32,1024]{1,0:T(8,128)} copy(f32[32,1024]{1,0:T(8,128)S(1)} %get-tuple-element.19) | data formatting | bytes 262144
Async XLA Ops:
  0.6 1.9 %copy-start = (bf16[2048,128]{1,0:T(8,128)(2,1)S(1)}, bf16[2048,128]{1,0:T(8,128)(2,1)}, u32[]{:S(2)}) copy-start(bf16[2048,128]{1,0:T(8,128)(2,1)} %field_ref.1) | copy-start | bytes 1572868
  0.6 1.9 %copy-start.1 = (f32[2,4,2048]{2,1,0:T(4,128)S(1)}, f32[2,4,2048]{2,1,0:T(4,128)}, u32[]{:S(2)}) copy-start(f32[2,4,2048]{2,1,0:T(4,128)} %coef_ref.1) | copy-start | bytes 196612
  0.7 1.9 %copy-start.2 = (s32[2048,4]{0,1:T(4,128)S(1)}, s32[2048,4]{0,1:T(4,128)}, u32[]{:S(2)}) copy-start(s32[2048,4]{0,1:T(4,128)} %param.10) | copy-start | bytes 98308
  0.7 1.9 %copy-start.3 = (s32[128,64]{0,1:T(8,128)S(1)}, s32[128,64]{0,1:T(8,128)}, u32[]{:S(2)}) copy-start(s32[128,64]{0,1:T(8,128)} %param.12) | copy-start | bytes 98308
  0.7 1.9 %copy-start.4 = (s32[128,32]{0,1:T(8,128)S(1)}, s32[128,32]{0,1:T(8,128)}, u32[]{:S(2)}) copy-start(s32[128,32]{0,1:T(8,128)} %param.13) | copy-start | bytes 49156
  0.7 1.9 %copy-start.6 = (s32[128,1]{0,1:T(1,128)S(1)}, s32[128,1]{0,1:T(1,128)}, u32[]{:S(2)}) copy-start(s32[128,1]{0,1:T(1,128)} %param.14) | copy-start | bytes 1540
  0.7 13.1 %copy-start.5 = (f32[8]{0:T(128)S(1)}, f32[8]{0:T(128)}, u32[]{:S(2)}) copy-start(f32[8]{0:T(128)} %level_ref.1) | copy-start | bytes 100

commit v5 on v4

--- a/solution.py
+++ b/solution.py
@@ -433,16 +433,19 @@
 
     @pl.loop(0, bands)
     def _(band):
-        total[...] = gather(steps - 1, band)
+        total[band] = gather(steps - 1, band)
+
+    @pl.loop(0, bands)
+    def _(band):
         line_copy(steps - 2, band, partner).wait_recv()
-        total[...] += dense_in[steps - 2, band].astype(jnp.float32)
+        total[band] += dense_in[steps - 2, band].astype(jnp.float32)
 
         @pl.loop(0, outers - 1)
         def _(turn):
             line_copy(2 * turn + 1, band, mirror(turn + 1)).wait_recv()
-            total[...] += dense_in[2 * turn + 1, band].astype(jnp.float32)
-
-        result = total[...]
+            total[band] += dense_in[2 * turn + 1, band].astype(jnp.float32)
+
+        result = total[band]
         remapped_ref[band] = result.astype(jnp.bfloat16)
         local_sum[band] = lax.dot_general(
             mix,
@@ -498,7 +501,7 @@
             pltpu.VMEM((steps, PLANE) + chunk, jnp.bfloat16),
             pltpu.VMEM((steps, PLANE) + chunk, jnp.bfloat16),
             pltpu.VMEM((PLANE, steps, SUB, LANES), jnp.int32),
-            pltpu.VMEM((BAND, columns), jnp.float32),
+            pltpu.VMEM(dense, jnp.float32),
             pltpu.VMEM((steps - 1,) + dense, jnp.bfloat16),
             pltpu.VMEM((steps - 1,) + dense, jnp.bfloat16),
             pltpu.VMEM((bands, FIELDS, BAND), jnp.float32),

time: 56.3 us -> 55.9 us (level)
  no operation moved by 1% of the time
where the time goes in v5:
time: 55.9 us; the launch traced here: 55.7 us
  Pallas kernels  51.8 us (93%)
  local copies, waits for them, and re-layouts  3.19 us (6%)
  between operations  0.77 us (1%)
    pallas_call x1, Pallas kernels, remap(): pl.pallas_call(functools.partial(remap_kernel, count, capacity, level_cou...  40.6 us
    pallas_call x1, Pallas kernels, prepare(): pl.pallas_call(functools.partial(prepare_kernel, count, lev_count, lines)...  11.2 us
    unnamed x17, local copies, waits for them, and re-layouts  3.19 us

profile of v5, /device:TPU:3, one launch (start us, length us, event | category | flops | bytes accessed | tf_op | source)
XLA Modules:
  0.0 55.7 jit_solution(16894271991335033351)
XLA Ops:
  0.6 0.0 copy-start
  0.6 0.0 copy-start.1
  0.7 0.0 copy-start.2
  0.7 0.0 copy-start.3
  0.7 0.0 copy-start.4
  0.7 0.0 copy-start.6
  0.7 0.0 copy-start.5
  0.7 1.8 %copy.10 = bf16[16,8,48,128]{3,2,1,0:T(8,128)(2,1)S(1)} copy(bf16[16,8,48,128]{3,1,2,0:T(8,128)(2,1)} %bitcast.17) | data formatting | bytes 3145728
  2.5 0.0 copy-done
  2.5 0.0 copy-done.1
  2.5 0.0 copy-done.2
  2.5 0.0 copy-done.3
  2.5 0.0 copy-done.4
  2.6 0.0 copy-done.6
  2.6 11.2 %prepare.1 = (f32[2,16384,128]{2,1,0:T(8,128)S(1)}, s32[8,64]{1,0:T(8,128)S(1)}, s32[8,128]{1,0:T(8,128)S(1)}, s32[128,128]{1,0:T(8,128)S(1)}, s32[64,64]{1,0:T(8,128)S(1)}) custom-call(bf16[2048,128]{1,0:T(8,128)(2,1)S(1)} %copy-done, f32[2,4,2048]{2,1,0:T(4,128)S(1)} %copy-done.1, s32[4,2048]{1,0:T(4,128)S(1)} %bitcast.13, s32[1,128]{1,0:T(1,128)S(1)} %bitcast.16, ...), custom_call_target="tpu_custom_call" | custom-call | tf_op jit(solution)/shard_map/prepare/pallas_call | solution.py:204
  13.8 0.0 copy-done.5
  13.8 40.6 %remap.1 = (bf16[4,256,128]{2,1,0:T(8,128)(2,1)S(1)}, f32[32,1024]{1,0:T(8,128)S(1)}) custom-call(s32[64,64]{1,0:T(8,128)S(1)} %get-tuple-element.9.src_ref, s32[8,64]{1,0:T(8,128)S(1)} %get-tuple-element.10.order_ref, s32[8,128]{1,0:T(8,128)S(1)} %get-tuple-element.11.start_ref, f32[8]{0:T(128)S(1)} %copy-done.5, f32[2,2048,8,128]{3,2,1,0:T(8,128)S(1)} %bitcast.9, ...), custom_call_target="tpu_custom_call" | custom-call | tf_op jit(solution)/shard_map/remap/pallas_call | solution.py:490
  54.4 0.7 %copy.13 = bf16[1024,128]{1,0:T(8,128)(2,1)} copy(bf16[1024,128]{1,0:T(8,128)(2,1)S(1)} %bitcast.11) | data formatting | bytes 524288
  55.1 0.7 %copy.14 = f32[32,1024]{1,0:T(8,128)} copy(f32[32,1024]{1,0:T(8,128)S(1)} %get-tuple-element.19) | data formatting | bytes 262144
Async XLA Ops:
  0.6 1.9 %copy-start = (bf16[2048,128]{1,0:T(8,128)(2,1)S(1)}, bf16[2048,128]{1,0:T(8,128)(2,1)}, u32[]{:S(2)}) copy-start(bf16[2048,128]{1,0:T(8,128)(2,1)} %field_ref.1) | copy-start | bytes 1572868
  0.6 1.9 %copy-start.1 = (f32[2,4,2048]{2,1,0:T(4,128)S(1)}, f32[2,4,2048]{2,1,0:T(4,128)}, u32[]{:S(2)}) copy-start(f32[2,4,2048]{2,1,0:T(4,128)} %coef_ref.1) | copy-start | bytes 196612
  0.7 1.9 %copy-start.2 = (s32[2048,4]{0,1:T(4,128)S(1)}, s32[2048,4]{0,1:T(4,128)}, u32[]{:S(2)}) copy-start(s32[2048,4]{0,1:T(4,128)} %param.10) | copy-start | bytes 98308
  0.7 1.9 %copy-start.3 = (s32[128,64]{0,1:T(8,128)S(1)}, s32[128,64]{0,1:T(8,128)}, u32[]{:S(2)}) copy-start(s32[128,64]{0,1:T(8,128)} %param.12) | copy-start | bytes 98308
  0.7 1.9 %copy-start.4 = (s32[128,32]{0,1:T(8,128)S(1)}, s32[128,32]{0,1:T(8,128)}, u32[]{:S(2)}) copy-start(s32[128,32]{0,1:T(8,128)} %param.13) | copy-start | bytes 49156
  0.7 1.9 %copy-start.6 = (s32[128,1]{0,1:T(1,128)S(1)}, s32[128,1]{0,1:T(1,128)}, u32[]{:S(2)}) copy-start(s32[128,1]{0,1:T(1,128)} %param.14) | copy-start | bytes 1540
  0.7 13.1 %copy-start.5 = (f32[8]{0:T(128)S(1)}, f32[8]{0:T(128)}, u32[]{:S(2)}) copy-start(f32[8]{0:T(128)} %level_ref.1) | copy-start | bytes 100
